TPU v7x, 512 devices: a whole 4x4x16 slice. The times are simulated.
512 devices in a mesh: wide: 128 (over z, y, core), narrow: 4 (over x).
Axes of the slice: x: 4, y: 4, z: 16, core: 2. Of those that a mesh axis runs over, the one named last changes fastest.
Arguments:
- level_rhs: float32 [128, 1024, 512], P('wide', 'narrow'), may hold values from -6 to 6
- galerkin_cols: int32 [7, 128, 16, 5], P(None, 'wide', 'narrow'), may hold values from 0 to 5, as said below
- galerkin_blocks: bfloat16 [7, 128, 16, 5, 64, 64], P(None, 'wide', 'narrow'), as said below
- restrict_cols: int32 [7, 128, 16, 3], P(None, 'wide', 'narrow'), may hold values from 0 to 7, as said below
- restrict_blocks: bfloat16 [7, 128, 16, 3, 64, 64], P(None, 'wide', 'narrow'), as said below
- prolong_cols: int32 [7, 128, 16, 2], P(None, 'wide', 'narrow'), may hold values from 0 to 3, as said below
- prolong_blocks: bfloat16 [7, 128, 16, 2, 64, 64], P(None, 'wide', 'narrow'), as said below
- coarse_inverse: bfloat16 [1024, 1024], P('narrow'), may hold values from -1.5 to 1.5
Outputs:
- correction: float32 [128, 1024, 512], P('wide', 'narrow')
Inputs may be any that keep to these rules, and one draw needn't show every extreme that they name: `galerkin_cols`: slot 0 of every block row names the row's own block; values below 4 name blocks of the same piece, 4 the last block of the piece before, 5 the first block of the piece after. At level k the entries of the 2**k subdomains of a group are equal. `galerkin_blocks`: at level k the blocks of the 2**k subdomains of a group are equal. The diagonal entries of every slot-0 block lie between 1 and 4. `restrict_cols`: values below 4 name blocks of the lower joined group, the others block value - 4 of the upper one; slots 0 and 1 of coarse block c name c and 4 + c. At level k the entries of the 2**(k+1) subdomains of a coarse group are equal. `restrict_blocks`: at level k the blocks of the 2**(k+1) subdomains of a coarse group are equal. `prolong_cols`: slot 0 names the fine block's own index. At level k the entries of the 2**k subdomains of a group are equal. `prolong_blocks`: at level k the blocks of the 2**k subdomains of a group are equal.
All inputs are finite; a program needn't handle non-finite values.
Results may differ from a plain program's by a relative error of at most 0.035.
Values may be sent and summed in bfloat16 or wider, within the bound.
A program may use at most 64 MiB of HBM per device.

v0:
```python
import jax
import jax.numpy as jnp
from jax import lax
from jax.sharding import PartitionSpec as P

relax_down = 0.7
relax_up = 0.5


def extended(cells, sides, width):
    for axis, dim in sides:
        count = lax.axis_size(axis)
        ends = count - 1
        head = lax.slice_in_dim(cells, 0, width, axis=dim)
        tail = lax.slice_in_dim(cells, cells.shape[dim] - width, cells.shape[dim], axis=dim)
        cells = jnp.concatenate(
            [
                lax.ppermute(tail, axis, [(i, (i + 1) % count) for i in range(ends)]),
                cells,
                lax.ppermute(head, axis, [((i + 1) % count, i) for i in range(ends)]),
            ],
            axis=dim,
        )
    return cells


def from_partner(value, axis, stride):
    return lax.ppermute(value, axis, [(i, i ^ 1 << stride) for i in range(lax.axis_size(axis))])


def block_apply(blocks, picked):
    return jnp.einsum("bsrc,bscn->brn", blocks, picked, preferred_element_type=jnp.float32)


def on_device(
    level_rhs,
    galerkin_cols,
    galerkin_blocks,
    restrict_cols,
    restrict_blocks,
    prolong_cols,
    prolong_blocks,
    coarse_inverse,
):
    level_count = galerkin_cols.shape[0]
    blocks_dev = galerkin_cols.shape[2]
    block_size = galerkin_blocks.shape[-1]
    fields = level_rhs.shape[-1]
    current = level_rhs[0].reshape(blocks_dev, block_size, fields)
    wide_index = lax.axis_index("wide")
    stored = []
    for level_idx in range(level_count):
        col_ids = galerkin_cols[level_idx, 0]
        blocks = galerkin_blocks[level_idx, 0]
        diagonal = jnp.diagonal(blocks[:, 0], axis1=-2, axis2=-1).astype(jnp.float32)[:, :, None]
        smoothed = relax_down * current / diagonal
        rounded = smoothed.astype(jnp.bfloat16)
        padded = extended(rounded, (("narrow", 0),), 1)
        mapped = jnp.where(
            col_ids < blocks_dev, col_ids + 1, jnp.where(col_ids == blocks_dev, 0, blocks_dev + 1)
        )
        applied = block_apply(blocks, padded[mapped])
        residual = (current - applied).astype(jnp.bfloat16)
        upper_bit = wide_index >> level_idx & 1
        rest_ids = restrict_cols[level_idx, 0]
        own_half = (rest_ids >= blocks_dev).astype(jnp.int32) == upper_bit
        within = rest_ids % blocks_dev
        partner = from_partner(residual, "wide", level_idx)
        picked = jnp.where(own_half[:, :, None, None], residual[within], partner[within])
        coarse_rhs = block_apply(restrict_blocks[level_idx, 0], picked)
        stored.append((current, smoothed, diagonal))
        current = coarse_rhs
    flat_rhs = current.astype(jnp.bfloat16).reshape(blocks_dev * block_size, fields)
    solution = jnp.dot(
        coarse_inverse,
        lax.all_gather(flat_rhs, "narrow", axis=0, tiled=True),
        preferred_element_type=jnp.float32,
    )
    current_x = solution.reshape(blocks_dev, block_size, fields)
    for level_idx in reversed(range(level_count)):
        fine_rhs, smoothed, diagonal = stored[level_idx]
        coarse_bf = current_x.astype(jnp.bfloat16)
        prolonged = block_apply(prolong_blocks[level_idx, 0], coarse_bf[prolong_cols[level_idx, 0]])
        updated = smoothed + prolonged
        updated_bf = updated.astype(jnp.bfloat16)
        col_ids = galerkin_cols[level_idx, 0]
        inside = col_ids < blocks_dev
        picked = jnp.where(
            inside[:, :, None, None],
            updated_bf[jnp.minimum(col_ids, blocks_dev - 1)],
            jnp.zeros((), jnp.bfloat16),
        )
        applied = block_apply(galerkin_blocks[level_idx, 0], picked)
        current_x = updated + relax_up * (fine_rhs - applied) / diagonal
    return current_x.reshape(1, blocks_dev * block_size, fields)


def solution(mesh):
    in_specs = (
        P("wide", "narrow", None),
        P(None, "wide", "narrow", None),
        P(None, "wide", "narrow", None, None, None),
        P(None, "wide", "narrow", None),
        P(None, "wide", "narrow", None, None, None),
        P(None, "wide", "narrow", None),
        P(None, "wide", "narrow", None, None, None),
        P("narrow", None),
    )
    out_specs = P("wide", "narrow", None)
    return jax.shard_map(
        on_device, mesh=mesh, in_specs=in_specs, out_specs=out_specs, check_vma=False
    )
```

profile of v0, /device:TPU:1, one launch (start us, length us, event | category | flops | bytes accessed | tf_op | source)
XLA Modules:
  0.0 338.9 jit_solution(1593955807330858841)
XLA Ops:
  6.5 2.7 slice_bitcast_fusion
  10.9 3.9 %collective-permute-start = (bf16[1,64,512]{2,1,0:T(8,128)(2,1)S(1)}, bf16[1,64,512]{2,1,0:T(8,128)(2,1)S(1)}, u32[]{:S(2)}, u32[]{:S(2)}) collective-permute-start(bf16[1,64,512]{2,1,0:T(8,128)(2,1)S(1)} %get-tuple-element.24), channel_id=1, source_target_pairs={{0,1},{1,2},{2,3},{4,5},{5,6},{6,7},{8,9},{9,10},{10,11},{12,13},{... | collective-permute-start | bytes 196616 | tf_op jit(solution)/shard_map/ppermute | solution.py:18
  44.4 1.8 gather_fusion.1
  46.2 1.9 fusion.146
  48.1 6.1 %collective-permute-start.2 = (bf16[4,64,512]{2,1,0:T(8,128)(2,1)S(1)}, bf16[4,64,512]{2,1,0:T(8,128)(2,1)S(1)}, u32[]{:S(2)}, u32[]{:S(2)}) collective-permute-start(bf16[4,64,512]{2,1,0:T(8,128)(2,1)S(1)} %fusion.146), channel_id=1, source_target_pairs={{0,4},{4,0},{8,12},{12,8},{16,20},{20,16},{24,28},{28,24},{32,36},... | collective-permute-start | bytes 786440 | tf_op jit(solution)/shard_map/ppermute | solution.py:28
  60.1 1.8 gather_fusion.2
  63.4 1.8 convolution_bitcast_fusion.20
  65.4 4.3 %collective-permute-start.3 = (bf16[1,64,512]{2,1,0:T(8,128)(2,1)S(1)}, bf16[1,64,512]{2,1,0:T(8,128)(2,1)S(1)}, u32[]{:S(2)}, u32[]{:S(2)}) collective-permute-start(bf16[1,64,512]{2,1,0:T(8,128)(2,1)S(1)} %get-tuple-element.22), channel_id=1, source_target_pairs={{0,1},{1,2},{2,3},{4,5},{5,6},{6,7},{8,9},{9,10},{10,11},{12,13},{... | collective-permute-start | bytes 196616 | tf_op jit(solution)/shard_map/ppermute | solution.py:18
  71.2 3.5 %collective-permute-done.4 = bf16[1,64,512]{2,1,0:T(8,128)(2,1)S(1)} collective-permute-done((bf16[1,64,512]{2,1,0:T(8,128)(2,1)S(1)}, bf16[1,64,512]{2,1,0:T(8,128)(2,1)S(1)}, u32[]{:S(2)}, u32[]{:S(2)}) %collective-permute-start.4) | collective-permute-done | bytes 65568 | tf_op jit(solution)/shard_map/ppermute | solution.py:20
  74.8 1.8 gather_fusion.5
  76.6 1.9 fusion.184
  78.4 1.9 collective-permute-start.5
  88.2 1.8 convolution_bitcast_fusion.19
  90.2 3.2 collective-permute-start.6
  95.3 3.1 collective-permute-done.7
  98.5 1.8 gather_fusion.9
  100.2 1.9 fusion.185
  102.1 1.9 collective-permute-start.8
  106.8 3.9 %collective-permute-done.8 = bf16[4,64,512]{2,1,0:T(8,128)(2,1)S(1)} collective-permute-done((bf16[4,64,512]{2,1,0:T(8,128)(2,1)S(1)}, bf16[4,64,512]{2,1,0:T(8,128)(2,1)S(1)}, u32[]{:S(2)}, u32[]{:S(2)}) %collective-permute-start.8) | collective-permute-done | bytes 262176 | tf_op jit(solution)/shard_map/ppermute | solution.py:28
  112.2 1.8 convolution_bitcast_fusion.18
  115.5 4.0 %collective-permute-start.9 = (bf16[1,64,512]{2,1,0:T(8,128)(2,1)S(1)}, bf16[1,64,512]{2,1,0:T(8,128)(2,1)S(1)}, u32[]{:S(2)}, u32[]{:S(2)}) collective-permute-start(bf16[1,64,512]{2,1,0:T(8,128)(2,1)S(1)} %get-tuple-element.18), channel_id=1, source_target_pairs={{0,1},{1,2},{2,3},{4,5},{5,6},{6,7},{8,9},{9,10},{10,11},{12,13},{... | collective-permute-start | bytes 196616 | tf_op jit(solution)/shard_map/ppermute | solution.py:18
  120.9 1.8 gather_fusion.13
  122.7 1.9 fusion.186
  124.6 1.9 collective-permute-start.11
  128.1 1.6 gather_fusion.20
  133.2 1.8 convolution_bitcast_fusion.17
  135.2 3.9 %collective-permute-start.12 = (bf16[1,64,512]{2,1,0:T(8,128)(2,1)S(1)}, bf16[1,64,512]{2,1,0:T(8,128)(2,1)S(1)}, u32[]{:S(2)}, u32[]{:S(2)}) collective-permute-start(bf16[1,64,512]{2,1,0:T(8,128)(2,1)S(1)} %get-tuple-element.16), channel_id=1, source_target_pairs={{0,1},{1,2},{2,3},{4,5},{5,6},{6,7},{8,9},{9,10},{10,11},{12,13},{... | collective-permute-start | bytes 196616 | tf_op jit(solution)/shard_map/ppermute | solution.py:18
  140.4 3.7 %collective-permute-done.13 = bf16[1,64,512]{2,1,0:T(8,128)(2,1)S(1)} collective-permute-done((bf16[1,64,512]{2,1,0:T(8,128)(2,1)S(1)}, bf16[1,64,512]{2,1,0:T(8,128)(2,1)S(1)}, u32[]{:S(2)}, u32[]{:S(2)}) %collective-permute-start.13) | collective-permute-done | bytes 65568 | tf_op jit(solution)/shard_map/ppermute | solution.py:20
  144.1 1.8 gather_fusion.17
  145.9 1.9 fusion.187
  147.8 3.0 collective-permute-start.14
  155.7 2.9 collective-permute-done.14
  160.1 1.8 convolution_bitcast_fusion.16
  162.1 2.5 collective-permute-start.15
  166.0 3.7 %collective-permute-done.16 = bf16[1,64,512]{2,1,0:T(8,128)(2,1)S(1)} collective-permute-done((bf16[1,64,512]{2,1,0:T(8,128)(2,1)S(1)}, bf16[1,64,512]{2,1,0:T(8,128)(2,1)S(1)}, u32[]{:S(2)}, u32[]{:S(2)}) %collective-permute-start.16) | collective-permute-done | bytes 65568 | tf_op jit(solution)/shard_map/ppermute | solution.py:20
  169.7 1.8 gather_fusion.21
  171.5 1.9 fusion.188
  173.4 8.1 %collective-permute-start.17 = (bf16[4,64,512]{2,1,0:T(8,128)(2,1)S(1)}, bf16[4,64,512]{2,1,0:T(8,128)(2,1)S(1)}, u32[]{:S(2)}, u32[]{:S(2)}) collective-permute-start(bf16[4,64,512]{2,1,0:T(8,128)(2,1)S(1)} %fusion.188), channel_id=1, source_target_pairs={{0,128},{4,132},{8,136},{12,140},{16,144},{20,148},{24,152},{28,15... | collective-permute-start | bytes 786440 | tf_op jit(solution)/shard_map/ppermute | solution.py:28
  183.5 18.8 %collective-permute-done.17 = bf16[4,64,512]{2,1,0:T(8,128)(2,1)S(1)} collective-permute-done((bf16[4,64,512]{2,1,0:T(8,128)(2,1)S(1)}, bf16[4,64,512]{2,1,0:T(8,128)(2,1)S(1)}, u32[]{:S(2)}, u32[]{:S(2)}) %collective-permute-start.17) | collective-permute-done | bytes 262176 | tf_op jit(solution)/shard_map/ppermute | solution.py:28
  203.8 1.8 convolution_bitcast_fusion.15
  205.8 2.2 collective-permute-start.18
  209.3 3.7 %collective-permute-done.19 = bf16[1,64,512]{2,1,0:T(8,128)(2,1)S(1)} collective-permute-done((bf16[1,64,512]{2,1,0:T(8,128)(2,1)S(1)}, bf16[1,64,512]{2,1,0:T(8,128)(2,1)S(1)}, u32[]{:S(2)}, u32[]{:S(2)}) %collective-permute-start.19) | collective-permute-done | bytes 65568 | tf_op jit(solution)/shard_map/ppermute | solution.py:20
  213.0 1.8 gather_fusion.25
  214.8 1.9 fusion.189
  216.7 11.5 %collective-permute-start.20 = (bf16[4,64,512]{2,1,0:T(8,128)(2,1)S(1)}, bf16[4,64,512]{2,1,0:T(8,128)(2,1)S(1)}, u32[]{:S(2)}, u32[]{:S(2)}) collective-permute-start(bf16[4,64,512]{2,1,0:T(8,128)(2,1)S(1)} %fusion.189), channel_id=1, source_target_pairs={{0,256},{4,260},{8,264},{12,268},{16,272},{20,276},{24,280},{28,28... | collective-permute-start | bytes 786440 | tf_op jit(solution)/shard_map/ppermute | solution.py:28
  229.9 2.9 collective-permute-done.20
  234.3 2.6 fusion.165
  237.1 39.5 %all-gather.2.cloned.1.call-done = bf16[1024,512]{1,0:T(8,128)(2,1)} async-done(((bf16[256,512]{1,0:T(8,128)(2,1)}), bf16[1024,512]{1,0:T(8,128)(2,1)}) %all-gather.2.cloned.1.call-update) | async-done | bytes 1048592 | tf_op jit(solution)/shard_map/all_gather | solution.py:76
  276.6 2.4 convolution_convert_fusion
  282.5 1.8 gather_fusion.29
  284.3 2.1 fusion.166
  290.1 1.8 gather_fusion.31
  291.8 2.7 fusion.169
  298.1 1.8 gather_fusion.33
  299.9 2.1 fusion.172
  305.6 1.8 gather_fusion.35
  307.4 2.7 fusion.175
  313.6 1.8 gather_fusion.37
  315.4 2.1 fusion.178
  321.1 1.8 gather_fusion.39
  322.9 1.9 fusion.181
  325.4 2.2 fusion.278
  327.6 1.8 gather_fusion.41
  329.3 2.7 fusion.123
  (410 shorter events, 101.8 us)
Async XLA Ops:
  6.5 270.1 %copy-start = (bf16[256,1024]{1,0:T(8,128)(2,1)S(1)}, bf16[256,1024]{1,0:T(8,128)(2,1)}, u32[]{:S(2)}) copy-start(bf16[256,1024]{1,0:T(8,128)(2,1)} %param.15) | copy-start | bytes 1572868
  6.5 270.1 %all-gather.2.cloned.1.call-start = ((), (), s32[]{:S(2)}) async-start(), calls=%async_computation | async-start | bytes 1310720 | tf_op jit(solution)/shard_map/all_gather | solution.py:76
  9.3 6.9 %copy-start.24 = (s32[7,1,4,3]{0,2,3,1:T(4,128)S(1)}, s32[7,1,4,3]{0,2,3,1:T(4,128)}, u32[]{:S(2)}) copy-start(s32[7,1,4,3]{0,2,3,1:T(4,128)} %param.11) | copy-start | bytes 1012
  9.3 8.1 %copy-start.23 = (s32[7,1,4,5]{0,2,3,1:T(4,128)S(1)}, s32[7,1,4,5]{0,2,3,1:T(4,128)}, u32[]{:S(2)}) copy-start(s32[7,1,4,5]{0,2,3,1:T(4,128)} %param.9) | copy-start | bytes 1684
  10.9 33.4 %collective-permute-start = (bf16[1,64,512]{2,1,0:T(8,128)(2,1)S(1)}, bf16[1,64,512]{2,1,0:T(8,128)(2,1)S(1)}, u32[]{:S(2)}, u32[]{:S(2)}) collective-permute-start(bf16[1,64,512]{2,1,0:T(8,128)(2,1)S(1)} %get-tuple-element.24), channel_id=1, source_target_pairs={{0,1},{1,2},{2,3},{4,5},{5,6},{6,7},{8,9},{9,10},{10,11},{12,13},{... | collective-permute-start | bytes 196616 | tf_op jit(solution)/shard_map/ppermute | solution.py:18
  14.9 29.4 %collective-permute-start.1 = (bf16[1,64,512]{2,1,0:T(8,128)(2,1)S(1)}, bf16[1,64,512]{2,1,0:T(8,128)(2,1)S(1)}, u32[]{:S(2)}, u32[]{:S(2)}) collective-permute-start(bf16[1,64,512]{2,1,0:T(8,128)(2,1)S(1)} %get-tuple-element.25), channel_id=1, source_target_pairs={{1,0},{2,1},{3,2},{5,4},{6,5},{7,6},{9,8},{10,9},{11,10},{13,12},{... | collective-permute-start | bytes 196616 | tf_op jit(solution)/shard_map/ppermute | solution.py:20
  16.3 17.1 %copy-start.26 = (s32[1,1,4,3]{0,2,3,1:T(4,128)}, s32[1,1,4,3]{0,2,3,1:T(4,128)S(1)}, u32[]{:S(2)}) copy-start(s32[1,1,4,3]{0,2,3,1:T(4,128)S(1)} %get-tuple-element.34) | copy-start | bytes 148
  20.5 15.4 %copy-start.25 = (s32[7,1,4,2]{0,3,2,1:T(2,128)S(1)}, s32[7,1,4,2]{0,3,2,1:T(2,128)}, u32[]{:S(2)}) copy-start(s32[7,1,4,2]{0,3,2,1:T(2,128)} %param.13) | copy-start | bytes 676
  22.0 22.3 %copy-start.28 = (s32[1,1,4,5]{3,2,1,0:T(4,128)}, s32[1,1,4,5]{3,2,1,0:T(4,128)S(1)}, u32[]{:S(2)}) copy-start(s32[1,1,4,5]{3,2,1,0:T(4,128)S(1)} %copy.222) | copy-start | bytes 244
  24.0 20.4 %copy-start.56 = (s32[1024]{0:T(1024)S(1)}, s32[1024]{0:T(1024)}, u32[]{:S(2)}) copy-start(s32[1024]{0:T(1024)} %pad_clamp_fusion.27) | copy-start | bytes 12292
  25.5 18.8 %copy-start.30 = (s32[1,1,4,5]{3,2,1,0:T(4,128)}, s32[1,1,4,5]{3,2,1,0:T(4,128)S(1)}, u32[]{:S(2)}) copy-start(s32[1,1,4,5]{3,2,1,0:T(4,128)S(1)} %copy.224) | copy-start | bytes 244
  27.7 16.6 %copy-start.32 = (s32[1,1,4,5]{3,2,1,0:T(4,128)}, s32[1,1,4,5]{3,2,1,0:T(4,128)S(1)}, u32[]{:S(2)}) copy-start(s32[1,1,4,5]{3,2,1,0:T(4,128)S(1)} %copy.226) | copy-start | bytes 244
  29.9 14.5 %copy-start.34 = (s32[1,1,4,5]{3,2,1,0:T(4,128)}, s32[1,1,4,5]{3,2,1,0:T(4,128)S(1)}, u32[]{:S(2)}) copy-start(s32[1,1,4,5]{3,2,1,0:T(4,128)S(1)} %copy.228) | copy-start | bytes 244
  32.0 12.3 %copy-start.36 = (s32[1,1,4,5]{3,2,1,0:T(4,128)}, s32[1,1,4,5]{3,2,1,0:T(4,128)S(1)}, u32[]{:S(2)}) copy-start(s32[1,1,4,5]{3,2,1,0:T(4,128)S(1)} %copy.230) | copy-start | bytes 244
  34.3 10.0 %copy-start.38 = (s32[1,1,4,5]{3,2,1,0:T(4,128)}, s32[1,1,4,5]{3,2,1,0:T(4,128)S(1)}, u32[]{:S(2)}) copy-start(s32[1,1,4,5]{3,2,1,0:T(4,128)S(1)} %copy.232) | copy-start | bytes 244
  46.2 8.0 %copy-start.83 = (s32[8]{0:T(128)S(1)}, s32[8]{0:T(128)}, u32[]{:S(2)}) copy-start(s32[8]{0:T(128)} %reshape.1517) | copy-start | bytes 100
  48.1 13.8 %collective-permute-start.2 = (bf16[4,64,512]{2,1,0:T(8,128)(2,1)S(1)}, bf16[4,64,512]{2,1,0:T(8,128)(2,1)S(1)}, u32[]{:S(2)}, u32[]{:S(2)}) collective-permute-start(bf16[4,64,512]{2,1,0:T(8,128)(2,1)S(1)} %fusion.146), channel_id=1, source_target_pairs={{0,4},{4,0},{8,12},{12,8},{16,20},{20,16},{24,28},{28,24},{32,36},... | collective-permute-start | bytes 786440 | tf_op jit(solution)/shard_map/ppermute | solution.py:28
  55.5 6.5 %copy-start.46 = (s32[1024]{0:T(1024)S(1)}, s32[1024]{0:T(1024)}, u32[]{:S(2)}) copy-start(s32[1024]{0:T(1024)} %pad_clamp_fusion.26) | copy-start | bytes 12292
  65.3 9.5 %copy-start.55 = (s32[1024]{0:T(1024)S(1)}, s32[1024]{0:T(1024)}, u32[]{:S(2)}) copy-start(s32[1024]{0:T(1024)} %pad_clamp_fusion.25) | copy-start | bytes 12292
  65.4 5.8 %collective-permute-start.3 = (bf16[1,64,512]{2,1,0:T(8,128)(2,1)S(1)}, bf16[1,64,512]{2,1,0:T(8,128)(2,1)S(1)}, u32[]{:S(2)}, u32[]{:S(2)}) collective-permute-start(bf16[1,64,512]{2,1,0:T(8,128)(2,1)S(1)} %get-tuple-element.22), channel_id=1, source_target_pairs={{0,1},{1,2},{2,3},{4,5},{5,6},{6,7},{8,9},{9,10},{10,11},{12,13},{... | collective-permute-start | bytes 196616 | tf_op jit(solution)/shard_map/ppermute | solution.py:18
  69.7 5.0 %collective-permute-start.4 = (bf16[1,64,512]{2,1,0:T(8,128)(2,1)S(1)}, bf16[1,64,512]{2,1,0:T(8,128)(2,1)S(1)}, u32[]{:S(2)}, u32[]{:S(2)}) collective-permute-start(bf16[1,64,512]{2,1,0:T(8,128)(2,1)S(1)} %get-tuple-element.23), channel_id=1, source_target_pairs={{1,0},{2,1},{3,2},{5,4},{6,5},{7,6},{9,8},{10,9},{11,10},{13,12},{... | collective-permute-start | bytes 196616 | tf_op jit(solution)/shard_map/ppermute | solution.py:20
  76.5 6.9 %copy-start.72 = (s32[4,5,1]{1,0,2:T(4,128)S(1)}, s32[4,5,1]{1,0,2:T(4,128)}, u32[]{:S(2)}) copy-start(s32[4,5,1]{1,0,2:T(4,128)} %get-tuple-element.57) | copy-start | bytes 244
  76.6 7.0 %copy-start.77 = (s32[4,2,1]{0,1,2:T(2,128)S(1)}, s32[4,2,1]{0,1,2:T(2,128)}, u32[]{:S(2)}) copy-start(s32[4,2,1]{0,1,2:T(2,128)} %compare_select_fusion.39) | copy-start | bytes 100
  76.6 7.2 %copy-start.45 = (s32[1024]{0:T(1024)S(1)}, s32[1024]{0:T(1024)}, u32[]{:S(2)}) copy-start(s32[1024]{0:T(1024)} %pad_clamp_fusion.24) | copy-start | bytes 12292
  78.4 8.3 %collective-permute-start.5 = (bf16[4,64,512]{2,1,0:T(8,128)(2,1)S(1)}, bf16[4,64,512]{2,1,0:T(8,128)(2,1)S(1)}, u32[]{:S(2)}, u32[]{:S(2)}) collective-permute-start(bf16[4,64,512]{2,1,0:T(8,128)(2,1)S(1)} %fusion.184), channel_id=1, source_target_pairs={{0,8},{4,12},{8,0},{12,4},{16,24},{20,28},{24,16},{28,20},{32,40},... | collective-permute-start | bytes 786440 | tf_op jit(solution)/shard_map/ppermute | solution.py:28
  80.4 9.6 %copy-start.61 = (f32[4,64]{1,0:T(4,128)}, f32[4,64]{1,0:T(4,128)S(1)}, u32[]{:S(2)}) copy-start(f32[4,64]{1,0:T(4,128)S(1)} %copy.148) | copy-start | bytes 3076
  90.0 8.4 %copy-start.54 = (s32[1024]{0:T(1024)S(1)}, s32[1024]{0:T(1024)}, u32[]{:S(2)}) copy-start(s32[1024]{0:T(1024)} %pad_clamp_fusion.23) | copy-start | bytes 12292
  90.2 5.1 %collective-permute-start.6 = (bf16[1,64,512]{2,1,0:T(8,128)(2,1)S(1)}, bf16[1,64,512]{2,1,0:T(8,128)(2,1)S(1)}, u32[]{:S(2)}, u32[]{:S(2)}) collective-permute-start(bf16[1,64,512]{2,1,0:T(8,128)(2,1)S(1)} %get-tuple-element.20), channel_id=1, source_target_pairs={{0,1},{1,2},{2,3},{4,5},{5,6},{6,7},{8,9},{9,10},{10,11},{12,13},{... | collective-permute-start | bytes 196616 | tf_op jit(solution)/shard_map/ppermute | solution.py:18
  93.4 5.0 %collective-permute-start.7 = (bf16[1,64,512]{2,1,0:T(8,128)(2,1)S(1)}, bf16[1,64,512]{2,1,0:T(8,128)(2,1)S(1)}, u32[]{:S(2)}, u32[]{:S(2)}) collective-permute-start(bf16[1,64,512]{2,1,0:T(8,128)(2,1)S(1)} %get-tuple-element.21), channel_id=1, source_target_pairs={{1,0},{2,1},{3,2},{5,4},{6,5},{7,6},{9,8},{10,9},{11,10},{13,12},{... | collective-permute-start | bytes 196616 | tf_op jit(solution)/shard_map/ppermute | solution.py:20
  102.1 8.6 %collective-permute-start.8 = (bf16[4,64,512]{2,1,0:T(8,128)(2,1)S(1)}, bf16[4,64,512]{2,1,0:T(8,128)(2,1)S(1)}, u32[]{:S(2)}, u32[]{:S(2)}) collective-permute-start(bf16[4,64,512]{2,1,0:T(8,128)(2,1)S(1)} %fusion.185), channel_id=1, source_target_pairs={{0,16},{4,20},{8,24},{12,28},{16,0},{20,4},{24,8},{28,12},{32,48},... | collective-permute-start | bytes 786440 | tf_op jit(solution)/shard_map/ppermute | solution.py:28
  104.1 9.9 %copy-start.63 = (f32[4,64]{1,0:T(4,128)}, f32[4,64]{1,0:T(4,128)S(1)}, u32[]{:S(2)}) copy-start(f32[4,64]{1,0:T(4,128)S(1)} %copy.154) | copy-start | bytes 3076
  105.3 6.9 %copy-start.80 = (pred[4,3]{1,0:T(4,128)(4,1)S(1)}, pred[4,3]{1,0:T(4,128)(4,1)}, u32[]{:S(2)}) copy-start(pred[4,3]{1,0:T(4,128)(4,1)} %fusion.242) | copy-start | bytes 40
  114.1 6.1 %copy-start.7 = (f32[4,512,64]{1,2,0:T(8,128)}, f32[4,512,64]{1,2,0:T(8,128)S(1)}, u32[]{:S(2)}) copy-start(f32[4,512,64]{1,2,0:T(8,128)S(1)} %convolution_bitcast_fusion.18) | copy-start | bytes 1572868
  114.1 6.8 %copy-start.52 = (s32[1024]{0:T(1024)S(1)}, s32[1024]{0:T(1024)}, u32[]{:S(2)}) copy-start(s32[1024]{0:T(1024)} %pad_clamp_fusion.21) | copy-start | bytes 12292
  114.2 5.9 %collective-permute-start.10 = (bf16[1,64,512]{2,1,0:T(8,128)(2,1)S(1)}, bf16[1,64,512]{2,1,0:T(8,128)(2,1)S(1)}, u32[]{:S(2)}, u32[]{:S(2)}) collective-permute-start(bf16[1,64,512]{2,1,0:T(8,128)(2,1)S(1)} %get-tuple-element.19), channel_id=1, source_target_pairs={{1,0},{2,1},{3,2},{5,4},{6,5},{7,6},{9,8},{10,9},{11,10},{13,12},{... | collective-permute-start | bytes 196616 | tf_op jit(solution)/shard_map/ppermute | solution.py:20
  115.5 5.3 %collective-permute-start.9 = (bf16[1,64,512]{2,1,0:T(8,128)(2,1)S(1)}, bf16[1,64,512]{2,1,0:T(8,128)(2,1)S(1)}, u32[]{:S(2)}, u32[]{:S(2)}) collective-permute-start(bf16[1,64,512]{2,1,0:T(8,128)(2,1)S(1)} %get-tuple-element.18), channel_id=1, source_target_pairs={{0,1},{1,2},{2,3},{4,5},{5,6},{6,7},{8,9},{9,10},{10,11},{12,13},{... | collective-permute-start | bytes 196616 | tf_op jit(solution)/shard_map/ppermute | solution.py:18
  122.7 6.9 %copy-start.70 = (s32[4,5,1]{1,0,2:T(4,128)S(1)}, s32[4,5,1]{1,0,2:T(4,128)}, u32[]{:S(2)}) copy-start(s32[4,5,1]{1,0,2:T(4,128)} %get-tuple-element.53) | copy-start | bytes 244
  122.7 7.0 %copy-start.75 = (s32[4,2,1]{0,1,2:T(2,128)S(1)}, s32[4,2,1]{0,1,2:T(2,128)}, u32[]{:S(2)}) copy-start(s32[4,2,1]{0,1,2:T(2,128)} %compare_select_fusion.37) | copy-start | bytes 100
  122.7 7.2 %copy-start.43 = (s32[1024]{0:T(1024)S(1)}, s32[1024]{0:T(1024)}, u32[]{:S(2)}) copy-start(s32[1024]{0:T(1024)} %pad_clamp_fusion.20) | copy-start | bytes 12292
  124.6 7.1 %collective-permute-start.11 = (bf16[4,64,512]{2,1,0:T(8,128)(2,1)S(1)}, bf16[4,64,512]{2,1,0:T(8,128)(2,1)S(1)}, u32[]{:S(2)}, u32[]{:S(2)}) collective-permute-start(bf16[4,64,512]{2,1,0:T(8,128)(2,1)S(1)} %fusion.186), channel_id=1, source_target_pairs={{0,32},{4,36},{8,40},{12,44},{16,48},{20,52},{24,56},{28,60},{32,0... | collective-permute-start | bytes 786440 | tf_op jit(solution)/shard_map/ppermute | solution.py:28
  126.6 8.4 %copy-start.65 = (f32[4,64]{1,0:T(4,128)}, f32[4,64]{1,0:T(4,128)S(1)}, u32[]{:S(2)}) copy-start(f32[4,64]{1,0:T(4,128)S(1)} %copy.160) | copy-start | bytes 3076
  135.0 9.1 %copy-start.50 = (s32[1024]{0:T(1024)S(1)}, s32[1024]{0:T(1024)}, u32[]{:S(2)}) copy-start(s32[1024]{0:T(1024)} %pad_clamp_fusion.19) | copy-start | bytes 12292
  135.2 5.2 %collective-permute-start.12 = (bf16[1,64,512]{2,1,0:T(8,128)(2,1)S(1)}, bf16[1,64,512]{2,1,0:T(8,128)(2,1)S(1)}, u32[]{:S(2)}, u32[]{:S(2)}) collective-permute-start(bf16[1,64,512]{2,1,0:T(8,128)(2,1)S(1)} %get-tuple-element.16), channel_id=1, source_target_pairs={{0,1},{1,2},{2,3},{4,5},{5,6},{6,7},{8,9},{9,10},{10,11},{12,13},{... | collective-permute-start | bytes 196616 | tf_op jit(solution)/shard_map/ppermute | solution.py:18
  139.1 5.0 %collective-permute-start.13 = (bf16[1,64,512]{2,1,0:T(8,128)(2,1)S(1)}, bf16[1,64,512]{2,1,0:T(8,128)(2,1)S(1)}, u32[]{:S(2)}, u32[]{:S(2)}) collective-permute-start(bf16[1,64,512]{2,1,0:T(8,128)(2,1)S(1)} %get-tuple-element.17), channel_id=1, source_target_pairs={{1,0},{2,1},{3,2},{5,4},{6,5},{7,6},{9,8},{10,9},{11,10},{13,12},{... | collective-permute-start | bytes 196616 | tf_op jit(solution)/shard_map/ppermute | solution.py:20
  145.9 8.0 %copy-start.69 = (s32[4,5,1]{1,0,2:T(4,128)S(1)}, s32[4,5,1]{1,0,2:T(4,128)}, u32[]{:S(2)}) copy-start(s32[4,5,1]{1,0,2:T(4,128)} %get-tuple-element.51) | copy-start | bytes 244
  145.9 8.1 %copy-start.74 = (s32[4,2,1]{0,1,2:T(2,128)S(1)}, s32[4,2,1]{0,1,2:T(2,128)}, u32[]{:S(2)}) copy-start(s32[4,2,1]{0,1,2:T(2,128)} %compare_select_fusion.36) | copy-start | bytes 100
  145.9 8.3 %copy-start.42 = (s32[1024]{0:T(1024)S(1)}, s32[1024]{0:T(1024)}, u32[]{:S(2)}) copy-start(s32[1024]{0:T(1024)} %pad_clamp_fusion.18) | copy-start | bytes 12292
  147.8 10.8 %collective-permute-start.14 = (bf16[4,64,512]{2,1,0:T(8,128)(2,1)S(1)}, bf16[4,64,512]{2,1,0:T(8,128)(2,1)S(1)}, u32[]{:S(2)}, u32[]{:S(2)}) collective-permute-start(bf16[4,64,512]{2,1,0:T(8,128)(2,1)S(1)} %fusion.187), channel_id=1, source_target_pairs={{0,64},{4,68},{8,72},{12,76},{16,80},{20,84},{24,88},{28,92},{32,9... | collective-permute-start | bytes 786440 | tf_op jit(solution)/shard_map/ppermute | solution.py:28
  162.0 7.7 %copy-start.49 = (s32[1024]{0:T(1024)S(1)}, s32[1024]{0:T(1024)}, u32[]{:S(2)}) copy-start(s32[1024]{0:T(1024)} %pad_clamp_fusion.17) | copy-start | bytes 12292
  162.1 3.8 %collective-permute-start.15 = (bf16[1,64,512]{2,1,0:T(8,128)(2,1)S(1)}, bf16[1,64,512]{2,1,0:T(8,128)(2,1)S(1)}, u32[]{:S(2)}, u32[]{:S(2)}) collective-permute-start(bf16[1,64,512]{2,1,0:T(8,128)(2,1)S(1)} %get-tuple-element.14), channel_id=1, source_target_pairs={{0,1},{1,2},{2,3},{4,5},{5,6},{6,7},{8,9},{9,10},{10,11},{12,13},{... | collective-permute-start | bytes 196616 | tf_op jit(solution)/shard_map/ppermute | solution.py:18
  164.6 5.0 %collective-permute-start.16 = (bf16[1,64,512]{2,1,0:T(8,128)(2,1)S(1)}, bf16[1,64,512]{2,1,0:T(8,128)(2,1)S(1)}, u32[]{:S(2)}, u32[]{:S(2)}) collective-permute-start(bf16[1,64,512]{2,1,0:T(8,128)(2,1)S(1)} %get-tuple-element.15), channel_id=1, source_target_pairs={{1,0},{2,1},{3,2},{5,4},{6,5},{7,6},{9,8},{10,9},{11,10},{13,12},{... | collective-permute-start | bytes 196616 | tf_op jit(solution)/shard_map/ppermute | solution.py:20
  171.5 10.0 %copy-start.27 = (s32[1,1,4,3]{0,2,3,1:T(4,128)S(1)}, s32[1,1,4,3]{0,2,3,1:T(4,128)}, u32[]{:S(2)}) copy-start(s32[1,1,4,3]{0,2,3,1:T(4,128)} %copy-done.26) | copy-start | bytes 148
  171.5 10.2 %copy-start.68 = (s32[4,5,1]{1,0,2:T(4,128)S(1)}, s32[4,5,1]{1,0,2:T(4,128)}, u32[]{:S(2)}) copy-start(s32[4,5,1]{1,0,2:T(4,128)} %get-tuple-element.49) | copy-start | bytes 244
  171.5 10.3 %copy-start.73 = (s32[4,2,1]{0,1,2:T(2,128)S(1)}, s32[4,2,1]{0,1,2:T(2,128)}, u32[]{:S(2)}) copy-start(s32[4,2,1]{0,1,2:T(2,128)} %compare_select_fusion.35) | copy-start | bytes 100
  171.5 10.5 %copy-start.40 = (s32[1024]{0:T(1024)S(1)}, s32[1024]{0:T(1024)}, u32[]{:S(2)}) copy-start(s32[1024]{0:T(1024)} %pad_clamp_fusion.16) | copy-start | bytes 12292
  173.4 28.9 %collective-permute-start.17 = (bf16[4,64,512]{2,1,0:T(8,128)(2,1)S(1)}, bf16[4,64,512]{2,1,0:T(8,128)(2,1)S(1)}, u32[]{:S(2)}, u32[]{:S(2)}) collective-permute-start(bf16[4,64,512]{2,1,0:T(8,128)(2,1)S(1)} %fusion.188), channel_id=1, source_target_pairs={{0,128},{4,132},{8,136},{12,140},{16,144},{20,148},{24,152},{28,15... | collective-permute-start | bytes 786440 | tf_op jit(solution)/shard_map/ppermute | solution.py:28
  205.6 7.4 %copy-start.48 = (s32[1024]{0:T(1024)S(1)}, s32[1024]{0:T(1024)}, u32[]{:S(2)}) copy-start(s32[1024]{0:T(1024)} %pad_clamp_fusion.15) | copy-start | bytes 12292
  205.8 3.5 %collective-permute-start.18 = (bf16[1,64,512]{2,1,0:T(8,128)(2,1)S(1)}, bf16[1,64,512]{2,1,0:T(8,128)(2,1)S(1)}, u32[]{:S(2)}, u32[]{:S(2)}) collective-permute-start(bf16[1,64,512]{2,1,0:T(8,128)(2,1)S(1)} %get-tuple-element.12), channel_id=1, source_target_pairs={{0,1},{1,2},{2,3},{4,5},{5,6},{6,7},{8,9},{9,10},{10,11},{12,13},{... | collective-permute-start | bytes 196616 | tf_op jit(solution)/shard_map/ppermute | solution.py:18
  208.0 5.0 %collective-permute-start.19 = (bf16[1,64,512]{2,1,0:T(8,128)(2,1)S(1)}, bf16[1,64,512]{2,1,0:T(8,128)(2,1)S(1)}, u32[]{:S(2)}, u32[]{:S(2)}) collective-permute-start(bf16[1,64,512]{2,1,0:T(8,128)(2,1)S(1)} %get-tuple-element.13), channel_id=1, source_target_pairs={{1,0},{2,1},{3,2},{5,4},{6,5},{7,6},{9,8},{10,9},{11,10},{13,12},{... | collective-permute-start | bytes 196616 | tf_op jit(solution)/shard_map/ppermute | solution.py:20
  214.8 13.5 %copy-start.67 = (s32[4,5,1]{1,0,2:T(4,128)S(1)}, s32[4,5,1]{1,0,2:T(4,128)}, u32[]{:S(2)}) copy-start(s32[4,5,1]{1,0,2:T(4,128)} %get-tuple-element.47) | copy-start | bytes 244
  214.8 13.6 %copy-start.41 = (s32[1024]{0:T(1024)S(1)}, s32[1024]{0:T(1024)}, u32[]{:S(2)}) copy-start(s32[1024]{0:T(1024)} %pad_clamp_fusion.14) | copy-start | bytes 12292
  216.7 16.1 %collective-permute-start.20 = (bf16[4,64,512]{2,1,0:T(8,128)(2,1)S(1)}, bf16[4,64,512]{2,1,0:T(8,128)(2,1)S(1)}, u32[]{:S(2)}, u32[]{:S(2)}) collective-permute-start(bf16[4,64,512]{2,1,0:T(8,128)(2,1)S(1)} %fusion.189), channel_id=1, source_target_pairs={{0,256},{4,260},{8,264},{12,268},{16,272},{20,276},{24,280},{28,28... | collective-permute-start | bytes 786440 | tf_op jit(solution)/shard_map/ppermute | solution.py:28
  236.9 42.1 %copy-start.47 = (s32[1024]{0:T(1024)S(1)}, s32[1024]{0:T(1024)}, u32[]{:S(2)}) copy-start(s32[1024]{0:T(1024)} %pad_clamp_fusion.13) | copy-start | bytes 12292
  237.1 43.4 %copy-start.14 = (f32[4,512,64]{1,2,0:T(8,128)S(1)}, f32[4,512,64]{1,2,0:T(8,128)}, u32[]{:S(2)}) copy-start(f32[4,512,64]{1,2,0:T(8,128)} %copy-done.13) | copy-start | bytes 1572868
  (42 other events, 129.9 us)
Sparse Core Ops, SparseCore 0:
  237.0 39.5 all-gather.1
where the time goes:
time: 341 us; the launch traced here: 339 us
  local copies, waits for them, and re-layouts  91.2 us (27%)
  waiting for transfers between devices  88.1 us (26%)
  starting transfers between devices  67.4 us (20%)
  matrix products  55.2 us (16%)
  other arithmetic  22.2 us (7%)
  between operations  14.8 us (4%)
    dot_general x28, matrix products, block_apply(): jnp.einsum('bsrc,bscn->brn', blocks, picked, preferred_element_type=jnp.f...  52.8 us
    all_gather x1, waiting for transfers between devices, on_device(): lax.all_gather(flat_rhs, 'narrow', axis=0, tiled=True)  39.5 us
    ppermute x7, starting transfers between devices, from_partner(): lax.ppermute(value, axis, [(i, i ^ 1 << stride) for i in range(lax.axis_s...  34.4 us
    ppermute x7, waiting for transfers between devices, from_partner(): lax.ppermute(value, axis, [(i, i ^ 1 << stride) for i in range(lax.axis_s...  30.1 us
    ppermute x7, starting transfers between devices, extended(): lax.ppermute(tail, axis, [(i, (i + 1) % count) for i in range(ends)])  24 us
    ppermute x7, waiting for transfers between devices, extended(): lax.ppermute(head, axis, [((i + 1) % count, i) for i in range(ends)])  17.7 us
    gather x7, local copies, waits for them, and re-layouts, on_device(): applied = block_apply(blocks, padded[mapped])  12.4 us
    gather x7, local copies, waits for them, and re-layouts, on_device(): updated_bf[jnp.minimum(col_ids, blocks_dev - 1)]  12.4 us
  transfers between devices with their start and end apart: 22, of which 14 were waited for; matrix products, arithmetic and copies ran while one was open for 17% of the time, Pallas kernels for 0%

commit v1 on v0

v1 whole, which is shorter than its diff:
```python
import jax
import jax.numpy as jnp
from jax import lax
from jax.experimental import pallas as pl
from jax.experimental.pallas import tpu as pltpu
from jax.sharding import PartitionSpec as P

relax_down = 0.7
relax_up = 0.5

LEVELS = 7
BS = 64
NB = 4
ROWS = NB * BS
CH = 128
STD = 2
SPLIT = (True, True, True, True, False, False, False)

f32 = jnp.float32
bf16 = jnp.bfloat16
NT = (((1,), (1,)), ((), ()))


def dot_nn(a, b):
    return jnp.dot(a, b, preferred_element_type=f32)


def dot_nt(a, b):
    return lax.dot_general(a, b, NT, preferred_element_type=f32)


def field_counts():
    counts = [4 * CH]
    for level in range(LEVELS):
        counts.append(counts[-1] // 2 if SPLIT[level] else counts[-1])
    return counts


FIELDS = field_counts()


def kernel(
    gcol, rcol, pcol, rhs_hbm, a_hbm, r_hbm, p_hbm, inv_hbm, out_hbm,
    b0, a_raw, r_raw, p_raw, cinv,
    a_own, a_halo, r_own, r_oth, p_own, dcol, drow,
    s0, s1, h0, h1, acc0, acc1, u0, u1, ro0, ro1, b1,
    bt, st, hs, hr, rt, ut, g_send, g_recv, xt, xq, x2o, x1b, x1r, outv,
    load_sem, out_sem, send_sem, recv_sem,
):
    w = lax.axis_index("wide")
    j = lax.axis_index("narrow")
    nxt = lax.rem(j + 1, 4)
    prv = lax.rem(j + 3, 4)
    bits = [lax.rem(w // (1 << k), 2) for k in range(LEVELS)]
    partners = [w + (1 - 2 * bits[k]) * (1 << k) for k in range(LEVELS)]

    barrier = pltpu.get_barrier_semaphore()
    for d in (1, 2, 3):
        pl.semaphore_signal(barrier, inc=1, device_id={"narrow": lax.rem(j + d, 4)})
    for k in range(LEVELS):
        pl.semaphore_signal(barrier, inc=1, device_id={"wide": partners[k]})

    own_q = bits[0] * 2 + bits[1]
    oth_q = bits[0] * 2 + (1 - bits[1])
    par_q = (1 - bits[0]) * 2 + bits[1]
    par_o = (1 - bits[0]) * 2 + (1 - bits[1])
    chunk = [par_o, par_q, oth_q, own_q]

    def lanes(slot):
        return pl.ds(pl.multiple_of(chunk[slot] * CH, CH), CH)

    n_load = [0]

    def load(src, dst):
        copy = pltpu.make_async_copy(src, dst, load_sem.at[n_load[0]])
        n_load[0] += 1
        copy.start()
        return copy

    ld_b = [load(rhs_hbm.at[0, :, lanes(i)], b0.at[i]) for i in range(2)]
    ld_a = {0: load(a_hbm.at[0, 0], a_raw.at[0])}
    ld_b += [load(rhs_hbm.at[0, :, lanes(i)], b0.at[i]) for i in (2, 3)]
    ld_r = {0: load(r_hbm.at[0, 0], r_raw.at[0])}
    ld_a[1] = load(a_hbm.at[1, 0], a_raw.at[1])
    ld_r[1] = load(r_hbm.at[1, 0], r_raw.at[1])
    for k in range(2, LEVELS):
        ld_a[k] = load(a_hbm.at[k, 0], a_raw.at[k])
        ld_r[k] = load(r_hbm.at[k, 0], r_raw.at[k])
    ld_p = load(p_hbm.at[:, 0], p_raw)
    ld_i = load(inv_hbm, cinv)

    n_rem = [0]

    def remote(src, dst, axis, where):
        idx = n_rem[0]
        n_rem[0] += 1
        return pltpu.make_async_remote_copy(
            src_ref=src, dst_ref=dst, send_sem=send_sem.at[idx], recv_sem=recv_sem.at[idx],
            device_id={axis: where}, device_id_type=pl.DeviceIdType.MESH,
        )

    started = []

    def go(copy):
        copy.start()
        started.append(copy)
        return copy

    lane = lax.broadcasted_iota(jnp.int32, (BS, 2 * BS), 1)
    row = lax.broadcasted_iota(jnp.int32, (BS, 2 * BS), 0)
    upper = lane // BS
    lo_code = jnp.where(j > 0, NB, -1)
    hi_code = jnp.where(j < 3, NB + 1, -1)
    halo_lo = jnp.where(upper == 0, lo_code, -1)
    halo_hi = jnp.where(upper == 1, hi_code, -1)
    halo_both = jnp.where(upper == 0, lo_code, hi_code)

    def doubled(block):
        wide = block.astype(f32)
        return jnp.concatenate([wide, wide], axis=1)

    def pick(code, ids, blocks):
        total = jnp.where(code == ids[0], blocks[0], 0.0)
        for c, blk in zip(ids[1:], blocks[1:]):
            total = total + jnp.where(code == c, blk, 0.0)
        return total.astype(bf16)

    def prep_a(k):
        ld_a[k].wait()

        def body(b, carry):
            at = pl.ds(pl.multiple_of(b * BS, BS), BS)
            ids = [gcol[k, 0, b, s] for s in range(5)]
            blocks = [doubled(a_raw[k, b, s]) for s in range(5)]
            a_own[k, at, 0:128] = pick(upper, ids, blocks)
            a_own[k, at, 128:256] = pick(upper + 2, ids, blocks)
            if k < STD:
                a_halo[k, at, 0:128] = pick(halo_both, ids, blocks)
            else:
                a_halo[k, at, 0:128] = pick(halo_lo, ids, blocks)
                a_halo[k, at, 128:256] = pick(halo_hi, ids, blocks)
            return carry

        lax.fori_loop(0, NB, body, 0)
        if k >= STD:
            for p in range(2):
                lo = doubled(a_raw[k, 2 * p, 0])
                hi = doubled(a_raw[k, 2 * p + 1, 0])
                diag = jnp.where(row == lane, lo, 0.0) + jnp.where(row + BS == lane, hi, 0.0)
                drow[k, 0:1, p * 128:(p + 1) * 128] = 1.0 / jnp.sum(diag, axis=0, keepdims=True)

    def prep_dcol(k):
        def body(b, carry):
            at = pl.ds(pl.multiple_of(b * BS, BS), BS)
            blk = doubled(a_raw[k, b, 0])
            d = jnp.sum(jnp.where(row == lane, blk, 0.0), axis=1, keepdims=True)
            dcol[k, at, :] = jnp.broadcast_to(1.0 / d, (BS, CH))
            return carry

        lax.fori_loop(0, NB, body, 0)

    def prep_r(k):
        ld_r[k].wait()

        def body(b, carry):
            at = pl.ds(pl.multiple_of(b * BS, BS), BS)
            ids = [rcol[k, 0, b, s] for s in range(3)]
            blocks = [doubled(r_raw[k, b, s]) for s in range(3)]
            for p in range(2):
                sl = slice(p * 128, (p + 1) * 128)
                r_own[k, at, sl] = pick(upper + (2 * p + NB * bits[k]), ids, blocks)
                r_oth[k, at, sl] = pick(upper + (2 * p + NB * (1 - bits[k])), ids, blocks)
            return carry

        lax.fori_loop(0, NB, body, 0)

    def prep_p(k):
        def body(b, carry):
            at = pl.ds(pl.multiple_of(b * BS, BS), BS)
            ids = [pcol[k, 0, b, s] for s in range(2)]
            blocks = [doubled(p_raw[k, b, s]) for s in range(2)]
            for p in range(2):
                p_own[k, at, p * 128:(p + 1) * 128] = pick(upper + 2 * p, ids, blocks)
            return carry

        lax.fori_loop(0, NB, body, 0)

    ld_a[0].wait()
    ld_a[0] = type("Done", (), {"wait": lambda self: None})()
    prep_dcol(0)
    sends_h0 = []
    for pair in range(2):
        for i in (2 * pair, 2 * pair + 1):
            ld_b[i].wait()
            s0[i] = (relax_down * b0[i] * dcol[0]).astype(bf16)
        if pair == 0:
            pl.semaphore_wait(barrier, 3 + LEVELS)
        at = pl.ds(2 * pair, 2)
        sends_h0.append((
            go(remote(s0.at[at, 192:256], h0.at[at, 0:64], "narrow", nxt)),
            go(remote(s0.at[at, 0:64], h0.at[at, 64:128], "narrow", prv)),
        ))
    prep_a(0)
    for i in range(4):
        acc0[i] = b0[i] - dot_nn(a_own[0], s0[i])
    for copy in sends_h0[0]:
        copy.wait_recv()
    ex0 = []
    for i in range(2):
        ro0[i] = (acc0[i] - dot_nn(a_halo[0, :, 0:128], h0[i])).astype(bf16)
        ex0.append(go(remote(ro0.at[i], u0.at[i], "wide", partners[0])))
    for copy in sends_h0[1]:
        copy.wait_recv()
    for i in (2, 3):
        ro0[i] = (acc0[i] - dot_nn(a_halo[0, :, 0:128], h0[i])).astype(bf16)
    prep_r(0)
    for i in range(2):
        acc1[i] = dot_nn(r_own[0], ro0[2 + i])
    ld_a[1].wait()
    ld_a[1] = ld_a[0]
    prep_dcol(1)
    sends_h1 = []
    for i in range(2):
        ex0[i].wait_recv()
        b1[i] = acc1[i] + dot_nn(r_oth[0], u0[i])
        s1[i] = (relax_down * b1[i] * dcol[1]).astype(bf16)
        sends_h1.append((
            go(remote(s1.at[i, 192:256], h1.at[i, 0:64], "narrow", nxt)),
            go(remote(s1.at[i, 0:64], h1.at[i, 64:128], "narrow", prv)),
        ))
    prep_a(1)
    for i in range(2):
        acc1[i] = b1[i] - dot_nn(a_own[1], s1[i])
    for i in range(2):
        for copy in sends_h1[i]:
            copy.wait_recv()
        ro1[i] = (acc1[i] - dot_nn(a_halo[1, :, 0:128], h1[i])).astype(bf16)
        if i == 0:
            ex1 = go(remote(ro1.at[0], u1, "wide", partners[1]))
    prep_r(1)
    part = dot_nn(r_own[1], ro1[1])
    acc1[1] = part
    prep_a(2)
    ex1.wait_recv()
    current = jnp.transpose(acc1[1] + dot_nn(r_oth[1], u1[...]))

    for k in range(STD, LEVELS):
        t = k - STD
        n = FIELDS[k]
        m = FIELDS[k + 1]
        bt[t, 0:n, :] = current
        smooth = relax_down * current * drow[k, 0:1, :]
        s_bf = smooth.astype(bf16)
        turned0 = pltpu.roll(smooth[:, 0:128], BS, 1)
        turned1 = pltpu.roll(smooth[:, 128:256], BS, 1)
        lane_n = lax.broadcasted_iota(jnp.int32, (n, 128), 1)
        hs[t, 0:n, :] = jnp.where(lane_n < BS, turned1, turned0).astype(bf16)
        send_a = go(remote(hs.at[t, 0:n], hr.at[t, 0:n, 0:128], "narrow", nxt))
        send_b = go(remote(hs.at[t, 0:n], hr.at[t, 0:n, 128:256], "narrow", prv))
        rest = current - dot_nt(s_bf, a_own[k])
        st[t, 0:n, :] = rest
        prep_r(k)
        send_a.wait_recv()
        send_b.wait_recv()
        rt[t, 0:n, :] = (st[t, 0:n, :] - dot_nt(hr[t, 0:n, :], a_halo[k])).astype(bf16)
        if SPLIT[k]:
            keep = pl.ds(pl.multiple_of(bits[k] * m, m), m)
            give = pl.ds(pl.multiple_of((1 - bits[k]) * m, m), m)
        else:
            keep = give = pl.ds(0, m)
        ex = go(remote(rt.at[t, give], ut.at[t, 0:m], "wide", partners[k]))
        bt[t + 1, 0:m, :] = dot_nt(rt[t, keep, :], r_own[k])
        if k + 1 < LEVELS:
            prep_a(k + 1)
        else:
            ld_p.wait()
            prep_p(6)
            ld_i.wait()
        ex.wait_recv()
        current = bt[t + 1, 0:m, :] + dot_nt(ut[t, 0:m, :], r_oth[k])

    n = FIELDS[LEVELS]
    g_send[...] = current.astype(bf16)
    gathers = [
        go(remote(g_send, g_recv.at[d - 1], "narrow", lax.rem(j + 4 - d, 4))) for d in (1, 2, 3)
    ]

    def inverse_cols(d):
        return cinv[:, pl.ds(pl.multiple_of(lax.rem(j + d, 4) * ROWS, ROWS), ROWS)]

    bt[LEVELS - STD, 0:n, :] = dot_nt(g_send[...], inverse_cols(0))
    for k in reversed(range(LEVELS - 1)):
        prep_p(k)
    for copy in gathers:
        copy.wait_recv()
    current = bt[LEVELS - STD, 0:n, :]
    for d in (1, 2, 3):
        current = current + dot_nt(g_recv[d - 1], inverse_cols(d))

    def up_rows(k, rows, x_bf):
        t = k - STD
        rhs = bt[t, rows, :]
        dinv = drow[k, 0:1, :]
        y = relax_down * rhs * dinv + dot_nt(x_bf, p_own[k])
        applied = dot_nt(y.astype(bf16), a_own[k])
        return y + relax_up * (rhs - applied) * dinv

    for k in reversed(range(STD, LEVELS)):
        t = k - STD
        n, m = FIELDS[k], FIELDS[k + 1]
        if SPLIT[k]:
            keep = pl.ds(pl.multiple_of(bits[k] * m, m), m)
            give = pl.ds(pl.multiple_of((1 - bits[k]) * m, m), m)
            xt[t, keep, :] = current.astype(bf16)
            ex = go(remote(xt.at[t, keep], xt.at[t, keep], "wide", partners[k]))
            xq[t, keep, :] = up_rows(k, keep, xt[t, keep, :])
            ex.wait_recv()
            xq[t, give, :] = up_rows(k, give, xt[t, give, :])
            current = xq[t, 0:n, :]
        else:
            current = up_rows(k, slice(0, n), current.astype(bf16))

    xt[LEVELS - STD, 0:CH, :] = current.astype(bf16)
    ex_up1 = go(remote(xt.at[LEVELS - STD, 0:CH], x2o, "wide", partners[1]))

    def up_cols(rhs, dinv, prolonged, a):
        y = relax_down * rhs * dinv + prolonged
        applied = dot_nn(a, y.astype(bf16))
        return y + relax_up * (rhs - applied) * dinv

    x1b[1] = up_cols(b1[1], dcol[1], dot_nt(p_own[1], xt[LEVELS - STD, 0:CH, :]), a_own[1]).astype(bf16)
    ex_up0 = [None, go(remote(x1b.at[1], x1r.at[1], "wide", partners[0]))]
    outs = []

    def finish(slot, x_bf):
        outv[slot] = up_cols(b0[slot], dcol[0], dot_nn(p_own[0], x_bf), a_own[0])
        copy = pltpu.make_async_copy(outv.at[slot], out_hbm.at[0, :, lanes(slot)], out_sem.at[slot])
        copy.start()
        outs.append(copy)

    ex_up1.wait_recv()
    x1b[0] = up_cols(b1[0], dcol[1], dot_nt(p_own[1], x2o[...]), a_own[1]).astype(bf16)
    ex_up0[0] = go(remote(x1b.at[0], x1r.at[0], "wide", partners[0]))
    finish(3, x1b[1])
    finish(2, x1b[0])
    for i in (1, 0):
        ex_up0[i].wait_recv()
        finish(i, x1r[i])
    for copy in started:
        copy.wait_send()
    for copy in outs:
        copy.wait()


REMOTES = 44


def on_device(*args):
    rhs, gcol, galerkin, rcol, restrict, pcol, prolong, inverse = args
    deep = LEVELS - STD
    top = FIELDS[STD]
    last = FIELDS[LEVELS]
    vmem = pltpu.VMEM
    scratch = [
        vmem((4, ROWS, CH), f32),
        vmem((LEVELS, NB, 5, BS, BS), bf16),
        vmem((LEVELS, NB, 3, BS, BS), bf16),
        vmem((LEVELS, NB, 2, BS, BS), bf16),
        vmem((ROWS, 4 * ROWS), bf16),
        vmem((LEVELS, ROWS, ROWS), bf16),
        vmem((LEVELS, ROWS, ROWS), bf16),
        vmem((LEVELS, ROWS, ROWS), bf16),
        vmem((LEVELS, ROWS, ROWS), bf16),
        vmem((LEVELS, ROWS, ROWS), bf16),
        vmem((STD, ROWS, CH), f32),
        vmem((LEVELS, 8, ROWS), f32),
        vmem((4, ROWS, CH), bf16),
        vmem((2, ROWS, CH), bf16),
        vmem((4, 2 * BS, CH), bf16),
        vmem((2, 2 * BS, CH), bf16),
        vmem((4, ROWS, CH), f32),
        vmem((2, ROWS, CH), f32),
        vmem((2, ROWS, CH), bf16),
        vmem((ROWS, CH), bf16),
        vmem((4, ROWS, CH), bf16),
        vmem((2, ROWS, CH), bf16),
        vmem((2, ROWS, CH), f32),
        vmem((deep + 1, top, ROWS), f32),
        vmem((deep, top, ROWS), f32),
        vmem((deep, top, 128), bf16),
        vmem((deep, top, ROWS), bf16),
        vmem((deep, top, ROWS), bf16),
        vmem((deep, top, ROWS), bf16),
        vmem((last, ROWS), bf16),
        vmem((3, last, ROWS), bf16),
        vmem((deep + 1, top, ROWS), bf16),
        vmem((deep, top, ROWS), f32),
        vmem((CH, ROWS), bf16),
        vmem((2, ROWS, CH), bf16),
        vmem((2, ROWS, CH), bf16),
        vmem((4, ROWS, CH), f32),
        pltpu.SemaphoreType.DMA((32,)),
        pltpu.SemaphoreType.DMA((4,)),
        pltpu.SemaphoreType.DMA((REMOTES,)),
        pltpu.SemaphoreType.DMA((REMOTES,)),
    ]
    smem = pl.BlockSpec(memory_space=pltpu.SMEM)
    hbm = pl.BlockSpec(memory_space=pl.ANY)
    return pl.pallas_call(
        kernel,
        out_shape=jax.ShapeDtypeStruct(rhs.shape, f32),
        in_specs=[smem, smem, smem, hbm, hbm, hbm, hbm, hbm],
        out_specs=hbm,
        scratch_shapes=scratch,
        compiler_params=pltpu.CompilerParams(
            collective_id=0, has_side_effects=True, vmem_limit_bytes=60 * 1024 * 1024
        ),
    )(gcol, rcol, pcol, rhs, galerkin, restrict, prolong, inverse)


def solution(mesh):
    in_specs = (
        P("wide", "narrow", None),
        P(None, "wide", "narrow", None),
        P(None, "wide", "narrow", None, None, None),
        P(None, "wide", "narrow", None),
        P(None, "wide", "narrow", None, None, None),
        P(None, "wide", "narrow", None),
        P(None, "wide", "narrow", None, None, None),
        P("narrow", None),
    )
    out_specs = P("wide", "narrow", None)
    return jax.shard_map(
        on_device, mesh=mesh, in_specs=in_specs, out_specs=out_specs, check_vma=False
    )
```

time: 341 us -> 93.2 us (0.27)
  waiting for transfers between devices: 88.1 us -> 0 us
  Pallas kernels: 0 us -> 86.8 us
  local copies, waits for them, and re-layouts: 91.2 us -> 6.03 us
  starting transfers between devices: 67.4 us -> 0 us
  matrix products: 55.2 us -> 0 us
  other arithmetic: 22.2 us -> 0 us
  between operations: 14.8 us -> 0.01 us
    pallas_call x0 -> x1, Pallas kernels: none -> 86.8 us  [on_device(): pl.pallas_call(kernel, out_shape=jax.ShapeDtypeStruct(rhs.shape, f32), in...]
    ppermute x21 -> x0, starting transfers between devices: 67.4 us -> none  [the longest x7 34.4 us: from_partner(): lax.ppermute(value, axis, [(i, i ^ 1 << stride) for i in range(lax.axis_s...]
    gather x42 -> x0, local copies, waits for them, and re-layouts: 64.3 us -> none  [the longest x7 12.4 us: on_device(): applied = block_apply(blocks, padded[mapped])]
    dot_general x29 -> x0, matrix products: 55.2 us -> none  [the longest x28 52.8 us: block_apply(): jnp.einsum('bsrc,bscn->brn', blocks, picked, preferred_element_type=jnp.f...]
    ppermute x21 -> x0, waiting for transfers between devices: 48.6 us -> none  [the longest x7 30.1 us: from_partner(): lax.ppermute(value, axis, [(i, i ^ 1 << stride) for i in range(lax.axis_s...]
    all_gather x1 -> x0, waiting for transfers between devices: 39.5 us -> none  [on_device(): lax.all_gather(flat_rhs, 'narrow', axis=0, tiled=True)]
    squeeze x12 -> x0, local copies, waits for them, and re-layouts: 12 us -> none  [the longest x11 9.3 us: on_device(): blocks[:, 0]]
    gather x28 -> x0, other arithmetic: 10.2 us -> none  [the longest x7 4.19 us: on_device(): applied = block_apply(blocks, padded[mapped])]
  transfers between devices with their start and end apart: 22 -> 0, of which waited for: 14 -> 0; matrix products, arithmetic and copies ran while one was open for 17% -> 0% of each run, Pallas kernels for 0% -> 0%
where the time goes in v1:
time: 93.2 us; the launch traced here: 92.8 us
  Pallas kernels  86.8 us (93%)
  local copies, waits for them, and re-layouts  6.03 us (6%)
    pallas_call x1, Pallas kernels, on_device(): pl.pallas_call(kernel, out_shape=jax.ShapeDtypeStruct(rhs.shape, f32), in...  86.8 us
    unnamed x4, local copies, waits for them, and re-layouts  6.03 us

profile of v1, /device:TPU:1, one launch (start us, length us, event | category | flops | bytes accessed | tf_op | source)
XLA Modules:
  0.0 92.8 jit_solution(3791998480898519025)
XLA Ops:
  0.0 1.4 %copy.9.gcol = s32[7,1,4,5]{3,2,1,0:T(4,128)} copy(s32[7,1,4,5]{0,2,3,1:T(4,128)} %param.9) | data formatting | bytes 1120 | tf_op args[1]
  1.4 1.4 %copy.10.rcol = s32[7,1,4,3]{3,2,1,0:T(4,128)} copy(s32[7,1,4,3]{0,2,3,1:T(4,128)} %param.11) | data formatting | bytes 672 | tf_op args[3]
  2.8 1.4 %copy.11.pcol = s32[7,1,4,2]{3,2,1,0:T(4,128)} copy(s32[7,1,4,2]{0,3,2,1:T(2,128)} %param.13) | data formatting | bytes 448 | tf_op args[5]
  4.2 86.8 %shard_map.82 = f32[1,256,512]{2,1,0:T(8,128)} custom-call(s32[7,1,4,5]{3,2,1,0:T(4,128)} %copy.9.gcol, s32[7,1,4,3]{3,2,1,0:T(4,128)} %copy.10.rcol, s32[7,1,4,2]{3,2,1,0:T(4,128)} %copy.11.pcol, f32[1,256,512]{2,1,0:T(8,128)} %rhs_hbm.1, bf16[7,1,4,5,64,64]{5,4,3,2,1,0:T(8,128)(2,1)} %a_hbm.1, bf16[7,1,4,3,64,64]{5,4,3,2,1,0:T(8,128)(2,1)} %r_hbm.1, ...), custom_call_target="tpu_custom_call" | custom-call | tf_op jit(solution)/shard_map/pallas_call | solution.py:409
  91.0 1.9 %copy.13 = f32[1,256,512]{2,1,0:T(8,128)} copy(f32[1,256,512]{2,1,0:T(8,128)} %shard_map.82) | data formatting | bytes 1048576

commit v2 on v0

v2 whole, which is shorter than its diff:
```python
import jax
import jax.numpy as jnp
from jax import lax
from jax.experimental import pallas as pl
from jax.experimental.pallas import tpu as pltpu
from jax.sharding import PartitionSpec as P

relax_down = 0.7
relax_up = 0.5

LEVELS = 7
SPLITS = 4
BS = 64
NB = 4
ROWS = NB * BS
ALL = 512
PIECES = 4
REMOTES = 96

f32 = jnp.float32
bf16 = jnp.bfloat16
NT = (((1,), (1,)), ((), ()))
FIELDS = [ALL >> min(level, SPLITS) for level in range(LEVELS + 1)]


def dot_nn(a, b):
    return jnp.dot(a, b, preferred_element_type=f32)


def dot_nt(a, b):
    return lax.dot_general(a, b, NT, preferred_element_type=f32)


def scratch_specs():
    vmem, dma = pltpu.VMEM, pltpu.SemaphoreType.DMA
    specs = {
        "gcol": pltpu.SMEM((1, 5, NB, LEVELS), jnp.int32),
        "rcol": pltpu.SMEM((1, 3, NB, LEVELS), jnp.int32),
        "pcol": pltpu.SMEM((1, NB, 2, LEVELS), jnp.int32),
        "b_std": vmem((ROWS, ALL), f32),
        "a_raw": vmem((LEVELS, NB, 5, BS, BS), bf16),
        "r_raw": vmem((LEVELS, NB, 3, BS, BS), bf16),
        "p_raw": vmem((LEVELS, NB, 2, BS, BS), bf16),
        "cinv": vmem((ROWS, PIECES * ROWS), bf16),
        "a_cat": vmem((LEVELS, ROWS, 2 * ROWS), bf16),
        "r_own": vmem((ROWS, ROWS), bf16),
        "p_own": vmem((ROWS, ROWS), bf16),
        "tmat": vmem((LEVELS, ROWS + 128, 2 * ROWS), bf16),
        "mmat": vmem((LEVELS, ROWS, ROWS), bf16),
        "deep": vmem((ROWS, ROWS), bf16),
        "fine": vmem((ROWS, ROWS), bf16),
        "kmat": vmem((ROWS, PIECES * ROWS), bf16),
        "drow": vmem((LEVELS, 8, ROWS), f32),
        "dcol": vmem((LEVELS, ROWS, 128), f32),
        "dsend": vmem((LEVELS, 8, 128), f32),
        "dhalo": vmem((2, LEVELS, 8, 128), f32),
        "h_send": vmem((ALL, 128), bf16),
        "h_recv": vmem((2, ALL, 128), bf16),
        "ctot": vmem((FIELDS[LEVELS], ROWS), f32),
        "c_std": vmem((ROWS, ALL), f32),
        "b7": vmem((PIECES, FIELDS[LEVELS], ROWS), bf16),
        "xg": vmem((ALL, ROWS), bf16),
        "outv": vmem((ROWS, ALL), f32),
        "load_sem": dma((32,)),
        "out_sem": dma((4,)),
        "send_sem": dma((REMOTES,)),
        "recv_sem": dma((REMOTES,)),
    }
    for k in range(LEVELS):
        n, m = FIELDS[k], FIELDS[k + 1]
        specs[f"bcat{k}"] = vmem((n, 2 * ROWS), bf16)
        specs[f"b32_{k + 1}"] = vmem((m, ROWS), f32)
        specs[f"pown{k}"] = vmem((m, ROWS), f32)
        specs[f"psend{k}"] = vmem((m, ROWS), bf16)
        specs[f"precv{k}"] = vmem((m, ROWS), bf16)
        if k < LEVELS - 1:
            specs[f"egive{k}"] = vmem((m, 128), bf16)
            specs[f"ekeep{k}"] = vmem((m, 128), bf16)
            specs[f"erecv{k}"] = vmem((4, m, 128), bf16)
        if 1 <= k < SPLITS:
            specs[f"cfull{k}"] = vmem((ALL, ROWS), bf16)
    return specs


class Refs:
    pass


def kernel(gcol_hbm, rcol_hbm, pcol_hbm, rhs_hbm, a_hbm, r_hbm, p_hbm, inv_hbm, out_hbm, *refs):
    v = Refs()
    for name, ref in zip(scratch_specs(), refs):
        setattr(v, name, ref)
    w = lax.axis_index("wide")
    j = lax.axis_index("narrow")
    nxt = lax.rem(j + 1, PIECES)
    prv = lax.rem(j + PIECES - 1, PIECES)
    has_next = j < PIECES - 1
    has_prev = j > 0
    bits = [lax.rem(w // (1 << k), 2) for k in range(LEVELS)]

    def across(mask):
        other = w
        for k in range(LEVELS):
            if mask >> k & 1:
                other = other + (1 - 2 * bits[k]) * (1 << k)
        return other

    partners = [across(1 << k) for k in range(LEVELS)]
    mates = range(1, 1 << SPLITS)

    barrier = pltpu.get_barrier_semaphore()
    greeted = [{"narrow": lax.rem(j + d, PIECES)} for d in (1, 2, 3)]
    greeted += [{"wide": p} for p in partners]
    greeted += [{"wide": p, "narrow": q} for p in partners[:-1] for q in (nxt, prv)]
    greeted += [{"wide": across(mask)} for mask in mates if mask & (mask - 1)]
    for where in greeted:
        pl.semaphore_signal(barrier, inc=1, device_id=where)

    n_load = [0]

    def load(src, dst):
        copy = pltpu.make_async_copy(src, dst, v.load_sem.at[n_load[0]])
        n_load[0] += 1
        copy.start()
        return copy

    ld_b = load(rhs_hbm.at[0], v.b_std)
    ld_g = load(gcol_hbm, v.gcol)
    ld_rc = load(rcol_hbm, v.rcol)
    ld_pc = load(pcol_hbm, v.pcol)
    ld_a0 = load(a_hbm.at[0, 0], v.a_raw.at[0])
    ld_r0 = load(r_hbm.at[0, 0], v.r_raw.at[0])
    rest = pl.ds(1, LEVELS - 1)
    ld_a = load(a_hbm.at[rest, 0], v.a_raw.at[rest])
    ld_r = load(r_hbm.at[rest, 0], v.r_raw.at[rest])
    ld_p = load(p_hbm.at[:, 0], v.p_raw)
    ld_i = load(inv_hbm, v.cinv)

    n_rem = [0]
    started = []

    def remote(src, dst, where, sends=None, recvs=None):
        idx = n_rem[0]
        n_rem[0] += 1
        copy = pltpu.make_async_remote_copy(
            src_ref=src, dst_ref=dst, send_sem=v.send_sem.at[idx], recv_sem=v.recv_sem.at[idx],
            device_id=where, device_id_type=pl.DeviceIdType.MESH,
        )
        if sends is None:
            copy.start()
        else:
            pl.when(sends)(copy.start)
        started.append((copy, sends))
        return copy, recvs

    def arrived(item):
        copy, recvs = item
        if recvs is None:
            copy.wait_recv()
        else:
            pl.when(recvs)(copy.wait_recv)

    lane = lax.broadcasted_iota(jnp.int32, (BS, 2 * BS), 1)
    row = lax.broadcasted_iota(jnp.int32, (BS, 2 * BS), 0)
    upper = lane // BS
    on_low = row == lane
    on_high = row + BS == lane
    halo_lo = jnp.where(upper == 0, jnp.where(has_prev, NB, -1), -1)
    halo_hi = jnp.where(upper == 1, jnp.where(has_next, NB + 1, -1), -1)

    def doubled(block):
        wide = block.astype(f32)
        return jnp.concatenate([wide, wide], axis=1)

    def pick(code, ids, blocks):
        total = jnp.where(code == ids[0], blocks[0], 0.0)
        for c, blk in zip(ids[1:], blocks[1:]):
            total = total + jnp.where(code == c, blk, 0.0)
        return total.astype(bf16)

    def each_block(body):
        def step(b, carry):
            body(b, pl.ds(pl.multiple_of(b * BS, BS), BS))
            return carry

        lax.fori_loop(0, NB, step, 0)

    def two_diagonals(k, low, high):
        picked = jnp.where(on_low, doubled(v.a_raw[k, low, 0]), 0.0)
        picked = picked + jnp.where(on_high, doubled(v.a_raw[k, high, 0]), 0.0)
        return 1.0 / jnp.sum(picked, axis=0, keepdims=True)

    def prep_diag(k):
        v.dsend[k] = jnp.broadcast_to(two_diagonals(k, 3, 0), (8, 128))
        v.drow[k, 0:1, 0:128] = two_diagonals(k, 0, 1)
        v.drow[k, 0:1, 128:256] = two_diagonals(k, 2, 3)

    def prep_t(k):
        def body(b, at):
            ids = [v.gcol[0, s, b, k] for s in range(5)]
            blocks = [doubled(v.a_raw[k, b, s]) for s in range(5)]
            v.a_cat[k, at, 0:128] = pick(upper, ids, blocks)
            v.a_cat[k, at, 128:256] = pick(upper + 2, ids, blocks)
            v.a_cat[k, at, 256:384] = pick(halo_lo, ids, blocks)
            v.a_cat[k, at, 384:512] = pick(halo_hi, ids, blocks)
            ids = [v.rcol[0, s, b, k] for s in range(3)]
            blocks = [doubled(v.r_raw[k, b, s]) for s in range(3)]
            v.r_own[at, 0:128] = pick(upper + NB * bits[k], ids, blocks)
            v.r_own[at, 128:256] = pick(upper + (2 + NB * bits[k]), ids, blocks)

        each_block(body)
        restrict = v.r_own[...]
        inner = dot_nn(restrict, v.a_cat[k, :, 0:256])
        own = (restrict.astype(f32) - relax_down * inner * v.drow[k, 0:1, :]).astype(bf16)
        v.tmat[k, 0:256, 0:256] = own
        v.tmat[k, 256:320, 0:256] = own[192:256]
        v.tmat[k, 320:384, 0:256] = own[0:64]
        outer = -relax_down * dot_nn(restrict, v.a_cat[k, :, 256:512])
        if k > 0:
            scale = jnp.concatenate([v.dhalo[0, k, 0:1, :], v.dhalo[1, k, 0:1, :]], axis=1)
            outer = outer * scale
        outer = outer.astype(bf16)
        v.tmat[k, 0:256, 256:512] = outer
        v.tmat[k, 256:320, 256:512] = outer[192:256]
        v.tmat[k, 320:384, 256:512] = outer[0:64]

    def prep_m(k):
        def body(b, at):
            ids = [v.pcol[0, b, s, k] for s in range(2)]
            blocks = [doubled(v.p_raw[k, b, s]) for s in range(2)]
            v.p_own[at, 0:128] = pick(upper, ids, blocks)
            v.p_own[at, 128:256] = pick(upper + 2, ids, blocks)
            d = jnp.sum(jnp.where(on_low, doubled(v.a_raw[k, b, 0]), 0.0), axis=1, keepdims=True)
            v.dcol[k, at, :] = jnp.broadcast_to(1.0 / d, (BS, 128))

        each_block(body)
        prolong = v.p_own[...]
        inner = dot_nn(v.a_cat[k, :, 0:256], prolong)
        scale = jnp.concatenate([v.dcol[k], v.dcol[k]], axis=1)
        v.mmat[k] = (prolong.astype(f32) - relax_up * scale * inner).astype(bf16)

    def smoothed_twice(k):
        b = v.__dict__[f"b32_{k}"][...]
        dinv = v.drow[k, 0:1, :]
        s = relax_down * b * dinv
        return s + relax_up * (b - dot_nt(s.astype(bf16), v.a_cat[k, :, 0:256])) * dinv

    def share(k):
        n, m = FIELDS[k], FIELDS[k + 1]
        if m == n:
            return pl.ds(0, n), pl.ds(0, n)
        keep = pl.ds(pl.multiple_of(bits[k] * m, m), m)
        give = pl.ds(pl.multiple_of((1 - bits[k]) * m, m), m)
        return keep, give

    def own_rows(k):
        start = 0
        for t in range(min(k, SPLITS)):
            start = start + bits[t] * FIELDS[t + 1]
        return pl.ds(pl.multiple_of(start, FIELDS[k]), FIELDS[k]) if k else pl.ds(0, ALL)

    def no_halo(side):
        v.h_recv[side] = jnp.zeros((ALL, 128), bf16)
        v.dhalo[side] = jnp.zeros((LEVELS, 8, 128), f32)
        for k in range(LEVELS - 1):
            ref = v.__dict__[f"erecv{k}"]
            zeros = jnp.zeros((FIELDS[k + 1], 128), bf16)
            ref[side] = zeros
            ref[2 + side] = zeros

    pl.when(j == 0)(lambda: no_halo(0))
    pl.when(j == PIECES - 1)(lambda: no_halo(1))

    ld_a0.wait()
    prep_diag(0)
    ld_b.wait()
    for c in range(4):
        cols = slice(c * 128, (c + 1) * 128)
        edge = jnp.concatenate([v.b_std[192:256, cols], v.b_std[0:64, cols]], axis=0)
        v.h_send[cols, :] = (jnp.transpose(edge) * v.dsend[0, 0:1, :]).astype(bf16)
    pl.semaphore_wait(barrier, len(greeted))
    halo = [
        remote(v.h_send, v.h_recv.at[0], {"narrow": nxt}, has_next, has_prev),
        remote(v.h_send, v.h_recv.at[1], {"narrow": prv}, has_prev, has_next),
    ]
    ld_a.wait()
    for k in range(1, LEVELS):
        prep_diag(k)
    diags = [
        remote(v.dsend, v.dhalo.at[0], {"narrow": nxt}, has_next, has_prev),
        remote(v.dsend, v.dhalo.at[1], {"narrow": prv}, has_prev, has_next),
    ]
    for c in range(4):
        cols = slice(c * 128, (c + 1) * 128)
        v.bcat0[cols, 0:256] = jnp.transpose(v.b_std[:, cols]).astype(bf16)
    ld_g.wait()
    ld_rc.wait()
    ld_r0.wait()
    prep_t(0)
    for item in halo:
        arrived(item)
    v.bcat0[:, 256:384] = v.h_recv[0]
    v.bcat0[:, 384:512] = v.h_recv[1]

    def idle_work(k):
        if k == 0:
            ld_r.wait()
            for item in diags:
                arrived(item)
        if k + 1 < LEVELS:
            prep_t(k + 1)
        if k == 0:
            ld_pc.wait()
            ld_p.wait()
        prep_m(k)
        if 1 <= k < SPLITS:
            c_bf = smoothed_twice(k).astype(bf16)
            v.__dict__[f"cfull{k}"][own_rows(k), :] = c_bf
        if k == SPLITS:
            v.ctot[...] = smoothed_twice(k)
            v.deep[...] = v.mmat[k]
        if k > SPLITS:
            v.ctot[...] += dot_nt(smoothed_twice(k).astype(bf16), v.deep[...])
            v.deep[...] = dot_nn(v.deep[...], v.mmat[k]).astype(bf16)
        if k == LEVELS - 1:
            ld_i.wait()
            v.kmat[...] = dot_nn(v.deep[...], v.cinv[...]).astype(bf16)

    shared = {}
    for k in range(LEVELS):
        n, m = FIELDS[k], FIELDS[k + 1]
        bcat, pown, psend, precv = (v.__dict__[f"{x}{k}"] for x in ("bcat", "pown", "psend", "precv"))
        keep, give = share(k)
        wide_out = ROWS + 128 if k < LEVELS - 1 else ROWS
        weights = v.tmat[k, 0:wide_out, :]
        there = {"wide": partners[k]}
        pieces = []
        p = dot_nt(bcat[give, :], weights)
        psend[...] = p[:, 0:ROWS].astype(bf16)
        if k < LEVELS - 1:
            egive, ekeep, erecv = (v.__dict__[f"{x}{k}"] for x in ("egive", "ekeep", "erecv"))
            egive[...] = p[:, ROWS:].astype(bf16)
            pieces.append(remote(egive, erecv.at[2], {"wide": partners[k], "narrow": nxt}, has_next, has_prev))
            pieces.append(remote(egive, erecv.at[3], {"wide": partners[k], "narrow": prv}, has_prev, has_next))
        pieces.append(remote(psend, precv, there))
        if m < n:
            p = dot_nt(bcat[keep, :], weights)
            if k < LEVELS - 1:
                ekeep[...] = p[:, ROWS:].astype(bf16)
                edge = ekeep
        elif k < LEVELS - 1:
            edge = egive
        if k < LEVELS - 1:
            pieces.append(remote(edge, erecv.at[0], {"narrow": nxt}, has_next, has_prev))
            pieces.append(remote(edge, erecv.at[1], {"narrow": prv}, has_prev, has_next))
        pown[...] = p[:, 0:ROWS]
        idle_work(k)
        if k == SPLITS:
            for t in range(1, SPLITS):
                rows = own_rows(t)
                ref = v.__dict__[f"cfull{t}"]
                shared[t] = [
                    remote(ref.at[rows], ref.at[rows], {"wide": across(mask)}) for mask in range(1, 1 << t)
                ]
        for item in pieces:
            arrived(item)
        total = pown[...] + precv[...].astype(f32)
        if k < LEVELS - 1:
            after = v.__dict__[f"bcat{k + 1}"]
            v.__dict__[f"b32_{k + 1}"][...] = total
            after[:, 0:256] = total.astype(bf16)
            after[:, 256:384] = (erecv[0].astype(f32) + erecv[2].astype(f32)).astype(bf16)
            after[:, 384:512] = (erecv[1].astype(f32) + erecv[3].astype(f32)).astype(bf16)
        else:
            v.b7[0] = total.astype(bf16)

    gathers = [
        remote(v.b7.at[0], v.b7.at[d], {"narrow": lax.rem(j + PIECES - d, PIECES)}) for d in (2, 1, 3)
    ]

    def inverse_cols(d):
        return v.kmat[:, pl.ds(pl.multiple_of(lax.rem(j + d, PIECES) * ROWS, ROWS), ROWS)]

    b = v.b_std[...]
    dinv = jnp.concatenate([v.dcol[0]] * 4, axis=1)
    s = relax_down * b * dinv
    v.c_std[...] = s + relax_up * (b - dot_nn(v.a_cat[0, :, 0:256], s.astype(bf16))) * dinv
    v.fine[...] = v.mmat[0]
    for t in range(1, SPLITS):
        for item in shared[t]:
            arrived(item)
        v.c_std[...] += dot_nt(v.fine[...], v.__dict__[f"cfull{t}"][...])
        v.fine[...] = dot_nn(v.fine[...], v.mmat[t]).astype(bf16)
    v.ctot[...] += dot_nt(v.b7[0], inverse_cols(0))
    for item in gathers:
        arrived(item)
    x = v.ctot[...]
    for d in (1, 2, 3):
        x = x + dot_nt(v.b7[d], inverse_cols(d))

    rows = own_rows(SPLITS)
    v.xg[rows, :] = x.astype(bf16)
    handed = [
        remote(v.xg.at[rows], v.xg.at[rows], {"wide": across(mask)}) for mask in reversed(mates)
    ]
    for item in handed:
        arrived(item)
    outs = []
    for c in range(4):
        cols = slice(c * 128, (c + 1) * 128)
        v.outv[:, cols] = v.c_std[:, cols] + dot_nt(v.fine[...], v.xg[cols, :])
        copy = pltpu.make_async_copy(v.outv.at[:, cols], out_hbm.at[0, :, cols], v.out_sem.at[c])
        copy.start()
        outs.append(copy)
    for copy, sends in started:
        if sends is None:
            copy.wait_send()
        else:
            pl.when(sends)(copy.wait_send)
    for copy in outs:
        copy.wait()


def on_device(rhs, gcol, galerkin, rcol, restrict, pcol, prolong, inverse):
    hbm = pl.BlockSpec(memory_space=pl.ANY)
    return pl.pallas_call(
        kernel,
        out_shape=jax.ShapeDtypeStruct(rhs.shape, f32),
        in_specs=[hbm] * 8,
        out_specs=hbm,
        scratch_shapes=list(scratch_specs().values()),
        compiler_params=pltpu.CompilerParams(
            collective_id=0, has_side_effects=True, vmem_limit_bytes=60 * 1024 * 1024
        ),
    )(
        jnp.transpose(gcol, (1, 3, 2, 0)),
        jnp.transpose(rcol, (1, 3, 2, 0)),
        jnp.transpose(pcol, (1, 2, 3, 0)),
        rhs, galerkin, restrict, prolong, inverse,
    )


def solution(mesh):
    in_specs = (
        P("wide", "narrow", None),
        P(None, "wide", "narrow", None),
        P(None, "wide", "narrow", None, None, None),
        P(None, "wide", "narrow", None),
        P(None, "wide", "narrow", None, None, None),
        P(None, "wide", "narrow", None),
        P(None, "wide", "narrow", None, None, None),
        P("narrow", None),
    )
    out_specs = P("wide", "narrow", None)
    return jax.shard_map(
        on_device, mesh=mesh, in_specs=in_specs, out_specs=out_specs, check_vma=False
    )
```

time: 341 us -> 67.9 us (0.20)
  local copies, waits for them, and re-layouts: 91.2 us -> 1.87 us
  waiting for transfers between devices: 88.1 us -> 0 us
  starting transfers between devices: 67.4 us -> 0 us
  Pallas kernels: 0 us -> 65.9 us
  matrix products: 55.2 us -> 0 us
  other arithmetic: 22.2 us -> 0 us
  between operations: 14.8 us -> 0.01 us
    ppermute x21 -> x0, starting transfers between devices: 67.4 us -> none  [the longest x7 34.4 us: from_partner(): lax.ppermute(value, axis, [(i, i ^ 1 << stride) for i in range(lax.axis_s...]
    pallas_call x0 -> x1, Pallas kernels: none -> 65.9 us  [on_device(): pl.pallas_call(kernel, out_shape=jax.ShapeDtypeStruct(rhs.shape, f32), in...]
    gather x42 -> x0, local copies, waits for them, and re-layouts: 64.3 us -> none  [the longest x7 12.4 us: on_device(): applied = block_apply(blocks, padded[mapped])]
    dot_general x29 -> x0, matrix products: 55.2 us -> none  [the longest x28 52.8 us: block_apply(): jnp.einsum('bsrc,bscn->brn', blocks, picked, preferred_element_type=jnp.f...]
    ppermute x21 -> x0, waiting for transfers between devices: 48.6 us -> none  [the longest x7 30.1 us: from_partner(): lax.ppermute(value, axis, [(i, i ^ 1 << stride) for i in range(lax.axis_s...]
    all_gather x1 -> x0, waiting for transfers between devices: 39.5 us -> none  [on_device(): lax.all_gather(flat_rhs, 'narrow', axis=0, tiled=True)]
    squeeze x12 -> x0, local copies, waits for them, and re-layouts: 12 us -> none  [the longest x11 9.3 us: on_device(): blocks[:, 0]]
    gather x28 -> x0, other arithmetic: 10.2 us -> none  [the longest x7 4.19 us: on_device(): applied = block_apply(blocks, padded[mapped])]
  transfers between devices with their start and end apart: 22 -> 0, of which waited for: 14 -> 0; matrix products, arithmetic and copies ran while one was open for 17% -> 0% of each run, Pallas kernels for 0% -> 0%
where the time goes in v2:
time: 67.9 us; the launch traced here: 67.8 us
  Pallas kernels  65.9 us (97%)
  local copies, waits for them, and re-layouts  1.87 us (3%)
    pallas_call x1, Pallas kernels, on_device(): pl.pallas_call(kernel, out_shape=jax.ShapeDtypeStruct(rhs.shape, f32), in...  65.9 us
    unnamed x1, local copies, waits for them, and re-layouts  1.87 us

profile of v2, /device:TPU:1, one launch (start us, length us, event | category | flops | bytes accessed | tf_op | source)
XLA Modules:
  0.0 67.8 jit_solution(9518346451069480458)
XLA Ops:
  0.0 65.9 %shard_map.82 = f32[1,256,512]{2,1,0:T(8,128)} custom-call(s32[1,5,4,7]{3,2,1,0:T(4,128)} %bitcast.3, s32[1,3,4,7]{3,2,1,0:T(4,128)} %bitcast.4, s32[1,4,2,7]{3,2,1,0:T(2,128)} %bitcast.5, f32[1,256,512]{2,1,0:T(8,128)} %rhs_hbm.1, bf16[7,1,4,5,64,64]{5,4,3,2,1,0:T(8,128)(2,1)} %a_hbm.1, bf16[7,1,4,3,64,64]{5,4,3,2,1,0:T(8,128)(2,1)} %r_hbm.1, ...), custom_call_target="tpu_custom_call" | custom-call | tf_op jit(solution)/shard_map/pallas_call | solution.py:426
  65.9 1.9 %copy.10 = f32[1,256,512]{2,1,0:T(8,128)} copy(f32[1,256,512]{2,1,0:T(8,128)} %shard_map.82) | data formatting | bytes 1048576

commit v3 on v2

--- a/solution.py
+++ b/solution.py
@@ -15,6 +15,7 @@
 ROWS = NB * BS
 ALL = 512
 PIECES = 4
+WIDE = ROWS + 2 * BS
 REMOTES = 96
 
 f32 = jnp.float32
@@ -42,20 +43,23 @@
         "r_raw": vmem((LEVELS, NB, 3, BS, BS), bf16),
         "p_raw": vmem((LEVELS, NB, 2, BS, BS), bf16),
         "cinv": vmem((ROWS, PIECES * ROWS), bf16),
-        "a_cat": vmem((LEVELS, ROWS, 2 * ROWS), bf16),
+        "a_cat": vmem((LEVELS, ROWS, WIDE), bf16),
         "r_own": vmem((ROWS, ROWS), bf16),
         "p_own": vmem((ROWS, ROWS), bf16),
-        "tmat": vmem((LEVELS, ROWS + 128, 2 * ROWS), bf16),
+        "tmat": vmem((LEVELS, WIDE, WIDE), bf16),
         "mmat": vmem((LEVELS, ROWS, ROWS), bf16),
         "deep": vmem((ROWS, ROWS), bf16),
         "fine": vmem((ROWS, ROWS), bf16),
-        "kmat": vmem((ROWS, PIECES * ROWS), bf16),
+        "kmat": vmem((PIECES * ROWS, ROWS), bf16),
         "drow": vmem((LEVELS, 8, ROWS), f32),
         "dcol": vmem((LEVELS, ROWS, 128), f32),
         "dsend": vmem((LEVELS, 8, 128), f32),
         "dhalo": vmem((2, LEVELS, 8, 128), f32),
-        "h_send": vmem((ALL, 128), bf16),
-        "h_recv": vmem((2, ALL, 128), bf16),
+        "edges": vmem((2 * BS, ALL), f32),
+        "edge_diag": vmem((2, BS, BS), bf16),
+        "h_send": vmem((2 * BS, ALL), bf16),
+        "h_recv": vmem((2 * BS, ALL), bf16),
+        "first": vmem((ALL, WIDE), f32),
         "ctot": vmem((FIELDS[LEVELS], ROWS), f32),
         "c_std": vmem((ROWS, ALL), f32),
         "b7": vmem((PIECES, FIELDS[LEVELS], ROWS), bf16),
@@ -65,10 +69,11 @@
         "out_sem": dma((4,)),
         "send_sem": dma((REMOTES,)),
         "recv_sem": dma((REMOTES,)),
+        "far_sem": pltpu.SemaphoreType.REGULAR((3, 2)),
     }
     for k in range(LEVELS):
         n, m = FIELDS[k], FIELDS[k + 1]
-        specs[f"bcat{k}"] = vmem((n, 2 * ROWS), bf16)
+        specs[f"bcat{k}"] = vmem((n, WIDE), bf16)
         specs[f"b32_{k + 1}"] = vmem((m, ROWS), f32)
         specs[f"pown{k}"] = vmem((m, ROWS), f32)
         specs[f"psend{k}"] = vmem((m, ROWS), bf16)
@@ -108,13 +113,25 @@
     partners = [across(1 << k) for k in range(LEVELS)]
     mates = range(1, 1 << SPLITS)
 
+    def ring(distance):
+        size = lax.axis_size("wide")
+        return lax.rem(w + distance, size), lax.rem(w + size - distance, size)
+
     barrier = pltpu.get_barrier_semaphore()
     greeted = [{"narrow": lax.rem(j + d, PIECES)} for d in (1, 2, 3)]
-    greeted += [{"wide": p} for p in partners]
-    greeted += [{"wide": p, "narrow": q} for p in partners[:-1] for q in (nxt, prv)]
-    greeted += [{"wide": across(mask)} for mask in mates if mask & (mask - 1)]
+    greeted += [{"wide": p} for p in partners[:3]]
+    greeted += [{"wide": p} for p in ring(8)]
     for where in greeted:
         pl.semaphore_signal(barrier, inc=1, device_id=where)
+
+    def pass_on(stage):
+        up, down = ring(8 << stage)
+        pl.semaphore_signal(v.far_sem.at[stage, 0], inc=1, device_id={"wide": up})
+        pl.semaphore_signal(v.far_sem.at[stage, 1], inc=1, device_id={"wide": down})
+
+    def passed(stage):
+        pl.semaphore_wait(v.far_sem.at[stage, 0], 1)
+        pl.semaphore_wait(v.far_sem.at[stage, 1], 1)
 
     n_load = [0]
 
@@ -124,6 +141,12 @@
         copy.start()
         return copy
 
+    ld_e = [
+        load(a_hbm.at[0, 0, 3, 0], v.edge_diag.at[0]),
+        load(a_hbm.at[0, 0, 0, 0], v.edge_diag.at[1]),
+        load(rhs_hbm.at[0, 192:256], v.edges.at[0:64]),
+        load(rhs_hbm.at[0, 0:64], v.edges.at[64:128]),
+    ]
     ld_b = load(rhs_hbm.at[0], v.b_std)
     ld_g = load(gcol_hbm, v.gcol)
     ld_rc = load(rcol_hbm, v.rcol)
@@ -165,8 +188,7 @@
     upper = lane // BS
     on_low = row == lane
     on_high = row + BS == lane
-    halo_lo = jnp.where(upper == 0, jnp.where(has_prev, NB, -1), -1)
-    halo_hi = jnp.where(upper == 1, jnp.where(has_next, NB + 1, -1), -1)
+    halo_code = jnp.where(upper == 0, jnp.where(has_prev, NB, -1), jnp.where(has_next, NB + 1, -1))
 
     def doubled(block):
         wide = block.astype(f32)
@@ -201,8 +223,7 @@
             blocks = [doubled(v.a_raw[k, b, s]) for s in range(5)]
             v.a_cat[k, at, 0:128] = pick(upper, ids, blocks)
             v.a_cat[k, at, 128:256] = pick(upper + 2, ids, blocks)
-            v.a_cat[k, at, 256:384] = pick(halo_lo, ids, blocks)
-            v.a_cat[k, at, 384:512] = pick(halo_hi, ids, blocks)
+            v.a_cat[k, at, 256:384] = pick(halo_code, ids, blocks)
             ids = [v.rcol[0, s, b, k] for s in range(3)]
             blocks = [doubled(v.r_raw[k, b, s]) for s in range(3)]
             v.r_own[at, 0:128] = pick(upper + NB * bits[k], ids, blocks)
@@ -210,19 +231,15 @@
 
         each_block(body)
         restrict = v.r_own[...]
-        inner = dot_nn(restrict, v.a_cat[k, :, 0:256])
-        own = (restrict.astype(f32) - relax_down * inner * v.drow[k, 0:1, :]).astype(bf16)
-        v.tmat[k, 0:256, 0:256] = own
-        v.tmat[k, 256:320, 0:256] = own[192:256]
-        v.tmat[k, 320:384, 0:256] = own[0:64]
-        outer = -relax_down * dot_nn(restrict, v.a_cat[k, :, 256:512])
+        inner = dot_nn(restrict, v.a_cat[k])
+        own = restrict.astype(f32) - relax_down * inner[:, 0:256] * v.drow[k, 0:1, :]
+        outer = -relax_down * inner[:, 256:384]
         if k > 0:
-            scale = jnp.concatenate([v.dhalo[0, k, 0:1, :], v.dhalo[1, k, 0:1, :]], axis=1)
-            outer = outer * scale
-        outer = outer.astype(bf16)
-        v.tmat[k, 0:256, 256:512] = outer
-        v.tmat[k, 256:320, 256:512] = outer[192:256]
-        v.tmat[k, 320:384, 256:512] = outer[0:64]
+            outer = outer * jnp.where(upper[0:1] == 0, v.dhalo[0, k, 0:1, :], v.dhalo[1, k, 0:1, :])
+        for at, part in ((slice(0, 128), own[:, 0:128]), (slice(128, 256), own[:, 128:256]), (slice(256, 384), outer)):
+            v.tmat[k, at, 0:256] = jnp.transpose(part).astype(bf16)
+            ends = jnp.concatenate([part[192:256], part[0:64]], axis=0)
+            v.tmat[k, at, 256:384] = jnp.transpose(ends).astype(bf16)
 
     def prep_m(k):
         def body(b, at):
@@ -260,7 +277,7 @@
         return pl.ds(pl.multiple_of(start, FIELDS[k]), FIELDS[k]) if k else pl.ds(0, ALL)
 
     def no_halo(side):
-        v.h_recv[side] = jnp.zeros((ALL, 128), bf16)
+        v.h_recv[side * BS:(side + 1) * BS, :] = jnp.zeros((BS, ALL), bf16)
         v.dhalo[side] = jnp.zeros((LEVELS, 8, 128), f32)
         for k in range(LEVELS - 1):
             ref = v.__dict__[f"erecv{k}"]
@@ -271,25 +288,27 @@
     pl.when(j == 0)(lambda: no_halo(0))
     pl.when(j == PIECES - 1)(lambda: no_halo(1))
 
-    ld_a0.wait()
-    prep_diag(0)
-    ld_b.wait()
-    for c in range(4):
-        cols = slice(c * 128, (c + 1) * 128)
-        edge = jnp.concatenate([v.b_std[192:256, cols], v.b_std[0:64, cols]], axis=0)
-        v.h_send[cols, :] = (jnp.transpose(edge) * v.dsend[0, 0:1, :]).astype(bf16)
+    for copy in ld_e:
+        copy.wait()
+    for i in range(2):
+        at = slice(i * BS, (i + 1) * BS)
+        d = jnp.sum(jnp.where(on_low, doubled(v.edge_diag[i]), 0.0), axis=1, keepdims=True)
+        v.h_send[at, :] = (v.edges[at, :] * (1.0 / d)).astype(bf16)
     pl.semaphore_wait(barrier, len(greeted))
     halo = [
-        remote(v.h_send, v.h_recv.at[0], {"narrow": nxt}, has_next, has_prev),
-        remote(v.h_send, v.h_recv.at[1], {"narrow": prv}, has_prev, has_next),
+        remote(v.h_send.at[0:64], v.h_recv.at[0:64], {"narrow": nxt}, has_next, has_prev),
+        remote(v.h_send.at[64:128], v.h_recv.at[64:128], {"narrow": prv}, has_prev, has_next),
     ]
+    pass_on(0)
+    ld_a0.wait()
     ld_a.wait()
-    for k in range(1, LEVELS):
+    for k in range(LEVELS):
         prep_diag(k)
     diags = [
         remote(v.dsend, v.dhalo.at[0], {"narrow": nxt}, has_next, has_prev),
         remote(v.dsend, v.dhalo.at[1], {"narrow": prv}, has_prev, has_next),
     ]
+    ld_b.wait()
     for c in range(4):
         cols = slice(c * 128, (c + 1) * 128)
         v.bcat0[cols, 0:256] = jnp.transpose(v.b_std[:, cols]).astype(bf16)
@@ -297,12 +316,18 @@
     ld_rc.wait()
     ld_r0.wait()
     prep_t(0)
+    v.first[...] = dot_nn(v.bcat0[:, 0:256], v.tmat[0, 0:256, :])
     for item in halo:
         arrived(item)
-    v.bcat0[:, 256:384] = v.h_recv[0]
-    v.bcat0[:, 384:512] = v.h_recv[1]
+    for c in range(4):
+        cols = slice(c * 128, (c + 1) * 128)
+        v.bcat0[cols, 256:384] = jnp.transpose(v.h_recv[:, cols].astype(f32)).astype(bf16)
 
     def idle_work(k):
+        if k < 3:
+            passed(k)
+            if k < 2:
+                pass_on(k + 1)
         if k == 0:
             ld_r.wait()
             for item in diags:
@@ -324,7 +349,9 @@
             v.deep[...] = dot_nn(v.deep[...], v.mmat[k]).astype(bf16)
         if k == LEVELS - 1:
             ld_i.wait()
-            v.kmat[...] = dot_nn(v.deep[...], v.cinv[...]).astype(bf16)
+            for d in range(PIECES):
+                at = slice(d * ROWS, (d + 1) * ROWS)
+                v.kmat[at, :] = jnp.transpose(dot_nn(v.deep[...], v.cinv[:, at])).astype(bf16)
 
     shared = {}
     for k in range(LEVELS):
@@ -332,10 +359,15 @@
         bcat, pown, psend, precv = (v.__dict__[f"{x}{k}"] for x in ("bcat", "pown", "psend", "precv"))
         keep, give = share(k)
         wide_out = ROWS + 128 if k < LEVELS - 1 else ROWS
-        weights = v.tmat[k, 0:wide_out, :]
+
+        def product(rows):
+            if k == 0:
+                return v.first[rows, :] + dot_nn(bcat[rows, 256:384], v.tmat[0, 256:384, :])
+            return dot_nn(bcat[rows, :], v.tmat[k, :, 0:wide_out])
+
         there = {"wide": partners[k]}
         pieces = []
-        p = dot_nt(bcat[give, :], weights)
+        p = product(give)
         psend[...] = p[:, 0:ROWS].astype(bf16)
         if k < LEVELS - 1:
             egive, ekeep, erecv = (v.__dict__[f"{x}{k}"] for x in ("egive", "ekeep", "erecv"))
@@ -344,7 +376,7 @@
             pieces.append(remote(egive, erecv.at[3], {"wide": partners[k], "narrow": prv}, has_prev, has_next))
         pieces.append(remote(psend, precv, there))
         if m < n:
-            p = dot_nt(bcat[keep, :], weights)
+            p = product(keep)
             if k < LEVELS - 1:
                 ekeep[...] = p[:, ROWS:].astype(bf16)
                 edge = ekeep
@@ -369,8 +401,10 @@
             after = v.__dict__[f"bcat{k + 1}"]
             v.__dict__[f"b32_{k + 1}"][...] = total
             after[:, 0:256] = total.astype(bf16)
-            after[:, 256:384] = (erecv[0].astype(f32) + erecv[2].astype(f32)).astype(bf16)
-            after[:, 384:512] = (erecv[1].astype(f32) + erecv[3].astype(f32)).astype(bf16)
+            before = erecv[0].astype(f32) + erecv[2].astype(f32)
+            behind = erecv[1].astype(f32) + erecv[3].astype(f32)
+            side = lax.broadcasted_iota(jnp.int32, (m, 128), 1)
+            after[:, 256:384] = jnp.where(side < BS, before, behind).astype(bf16)
         else:
             v.b7[0] = total.astype(bf16)
 
@@ -378,8 +412,8 @@
         remote(v.b7.at[0], v.b7.at[d], {"narrow": lax.rem(j + PIECES - d, PIECES)}) for d in (2, 1, 3)
     ]
 
-    def inverse_cols(d):
-        return v.kmat[:, pl.ds(pl.multiple_of(lax.rem(j + d, PIECES) * ROWS, ROWS), ROWS)]
+    def inverse_rows(d):
+        return v.kmat[pl.ds(pl.multiple_of(lax.rem(j + d, PIECES) * ROWS, ROWS), ROWS), :]
 
     b = v.b_std[...]
     dinv = jnp.concatenate([v.dcol[0]] * 4, axis=1)
@@ -391,12 +425,12 @@
             arrived(item)
         v.c_std[...] += dot_nt(v.fine[...], v.__dict__[f"cfull{t}"][...])
         v.fine[...] = dot_nn(v.fine[...], v.mmat[t]).astype(bf16)
-    v.ctot[...] += dot_nt(v.b7[0], inverse_cols(0))
+    v.ctot[...] += dot_nn(v.b7[0], inverse_rows(0))
     for item in gathers:
         arrived(item)
     x = v.ctot[...]
     for d in (1, 2, 3):
-        x = x + dot_nt(v.b7[d], inverse_cols(d))
+        x = x + dot_nn(v.b7[d], inverse_rows(d))
 
     rows = own_rows(SPLITS)
     v.xg[rows, :] = x.astype(bf16)

time: 67.9 us -> 63.8 us (0.940)
  Pallas kernels: 65.9 us -> 61.8 us
    pallas_call x1, Pallas kernels: 65.9 us -> 61.8 us  [on_device(): pl.pallas_call(kernel, out_shape=jax.ShapeDtypeStruct(rhs.shape, f32), in...]
where the time goes in v3:
time: 63.8 us; the launch traced here: 63.7 us
  Pallas kernels  61.8 us (97%)
  local copies, waits for them, and re-layouts  1.87 us (3%)
    pallas_call x1, Pallas kernels, on_device(): pl.pallas_call(kernel, out_shape=jax.ShapeDtypeStruct(rhs.shape, f32), in...  61.8 us
    unnamed x1, local copies, waits for them, and re-layouts  1.87 us

profile of v3, /device:TPU:1, one launch (start us, length us, event | category | flops | bytes accessed | tf_op | source)
XLA Modules:
  0.0 63.7 jit_solution(6063681102554904635)
XLA Ops:
  0.0 61.8 %shard_map.82 = f32[1,256,512]{2,1,0:T(8,128)} custom-call(s32[1,5,4,7]{3,2,1,0:T(4,128)} %bitcast.3, s32[1,3,4,7]{3,2,1,0:T(4,128)} %bitcast.4, s32[1,4,2,7]{3,2,1,0:T(2,128)} %bitcast.5, f32[1,256,512]{2,1,0:T(8,128)} %rhs_hbm.1, bf16[7,1,4,5,64,64]{5,4,3,2,1,0:T(8,128)(2,1)} %a_hbm.1, bf16[7,1,4,3,64,64]{5,4,3,2,1,0:T(8,128)(2,1)} %r_hbm.1, ...), custom_call_target="tpu_custom_call" | custom-call | tf_op jit(solution)/shard_map/pallas_call | solution.py:460
  61.8 1.9 %copy.10 = f32[1,256,512]{2,1,0:T(8,128)} copy(f32[1,256,512]{2,1,0:T(8,128)} %shard_map.82) | data formatting | bytes 1048576

commit v4 on v3

--- a/solution.py
+++ b/solution.py
@@ -10,6 +10,8 @@
 
 LEVELS = 7
 SPLITS = 4
+LAST = LEVELS - 1
+JOINED = LEVELS - 2
 BS = 64
 NB = 4
 ROWS = NB * BS
@@ -50,7 +52,10 @@
         "mmat": vmem((LEVELS, ROWS, ROWS), bf16),
         "deep": vmem((ROWS, ROWS), bf16),
         "fine": vmem((ROWS, ROWS), bf16),
-        "kmat": vmem((PIECES * ROWS, ROWS), bf16),
+        "deep_t": vmem((ROWS, ROWS), bf16),
+        "last_t": vmem((PIECES, WIDE, ROWS), bf16),
+        "zpart": vmem((PIECES, WIDE, ROWS), f32),
+        "zmat": vmem((PIECES, ROWS, ROWS), bf16),
         "drow": vmem((LEVELS, 8, ROWS), f32),
         "dcol": vmem((LEVELS, ROWS, 128), f32),
         "dsend": vmem((LEVELS, 8, 128), f32),
@@ -62,7 +67,12 @@
         "first": vmem((ALL, WIDE), f32),
         "ctot": vmem((FIELDS[LEVELS], ROWS), f32),
         "c_std": vmem((ROWS, ALL), f32),
-        "b7": vmem((PIECES, FIELDS[LEVELS], ROWS), bf16),
+        "q_all": vmem((PIECES, FIELDS[LEVELS], ROWS), bf16),
+        "q_own": vmem((FIELDS[LEVELS], ROWS), f32),
+        "q_far": vmem((FIELDS[LEVELS], ROWS), bf16),
+        "x_own": vmem((FIELDS[LEVELS], ROWS), f32),
+        "x_send": vmem((FIELDS[LEVELS], ROWS), bf16),
+        "x_recv": vmem((3, FIELDS[LEVELS], ROWS), bf16),
         "xg": vmem((ALL, ROWS), bf16),
         "outv": vmem((ROWS, ALL), f32),
         "load_sem": dma((32,)),
@@ -73,12 +83,14 @@
     }
     for k in range(LEVELS):
         n, m = FIELDS[k], FIELDS[k + 1]
-        specs[f"bcat{k}"] = vmem((n, WIDE), bf16)
-        specs[f"b32_{k + 1}"] = vmem((m, ROWS), f32)
-        specs[f"pown{k}"] = vmem((m, ROWS), f32)
-        specs[f"psend{k}"] = vmem((m, ROWS), bf16)
-        specs[f"precv{k}"] = vmem((m, ROWS), bf16)
-        if k < LEVELS - 1:
+        if k > 0:
+            specs[f"b32_{k}"] = vmem((n, ROWS), f32)
+        if k < LAST:
+            specs[f"bcat{k}"] = vmem((n, WIDE), bf16)
+        if k < JOINED:
+            specs[f"pown{k}"] = vmem((m, ROWS), f32)
+            specs[f"psend{k}"] = vmem((m, ROWS), bf16)
+            specs[f"precv{k}"] = vmem((m, ROWS), bf16)
             specs[f"egive{k}"] = vmem((m, 128), bf16)
             specs[f"ekeep{k}"] = vmem((m, 128), bf16)
             specs[f"erecv{k}"] = vmem((4, m, 128), bf16)
@@ -279,7 +291,7 @@
     def no_halo(side):
         v.h_recv[side * BS:(side + 1) * BS, :] = jnp.zeros((BS, ALL), bf16)
         v.dhalo[side] = jnp.zeros((LEVELS, 8, 128), f32)
-        for k in range(LEVELS - 1):
+        for k in range(JOINED):
             ref = v.__dict__[f"erecv{k}"]
             zeros = jnp.zeros((FIELDS[k + 1], 128), bf16)
             ref[side] = zeros
@@ -332,8 +344,11 @@
             ld_r.wait()
             for item in diags:
                 arrived(item)
-        if k + 1 < LEVELS:
+        if k + 1 < LAST:
             prep_t(k + 1)
+        if k == 0:
+            prep_t(LAST)
+            v.last_t[0] = v.tmat[LAST, :, 0:256]
         if k == 0:
             ld_pc.wait()
             ld_p.wait()
@@ -347,45 +362,61 @@
         if k > SPLITS:
             v.ctot[...] += dot_nt(smoothed_twice(k).astype(bf16), v.deep[...])
             v.deep[...] = dot_nn(v.deep[...], v.mmat[k]).astype(bf16)
-        if k == LEVELS - 1:
+        if k == JOINED - 1:
             ld_i.wait()
-            for d in range(PIECES):
-                at = slice(d * ROWS, (d + 1) * ROWS)
-                v.kmat[at, :] = jnp.transpose(dot_nn(v.deep[...], v.cinv[:, at])).astype(bf16)
-
+            for item in last_t:
+                arrived(item)
+            join_last()
+        if k == LAST:
+            v.deep_t[...] = jnp.transpose(v.deep[...].astype(f32)).astype(bf16)
+
+    def join_last():
+        for d in range(PIECES):
+            cols = pl.ds(pl.multiple_of(lax.rem(j + d, PIECES) * ROWS, ROWS), ROWS)
+            v.zpart[d] = dot_nt(v.last_t[d], v.cinv[:, cols])
+        for d in range(PIECES):
+            before, after = (d + PIECES - 1) % PIECES, (d + 1) % PIECES
+            v.zmat[d, 0:64, :] = (v.zpart[d, 0:64, :] + v.zpart[before, 320:384, :]).astype(bf16)
+            v.zmat[d, 64:192, :] = v.zpart[d, 64:192, :].astype(bf16)
+            v.zmat[d, 192:256, :] = (v.zpart[d, 192:256, :] + v.zpart[after, 256:320, :]).astype(bf16)
+
+    def to_pieces(ref, d):
+        return remote(ref.at[0], ref.at[d], {"narrow": lax.rem(j + PIECES - d, PIECES)})
+
+    last_t = []
     shared = {}
-    for k in range(LEVELS):
+    for k in range(JOINED):
         n, m = FIELDS[k], FIELDS[k + 1]
-        bcat, pown, psend, precv = (v.__dict__[f"{x}{k}"] for x in ("bcat", "pown", "psend", "precv"))
+        bcat, pown, psend, precv, egive, ekeep, erecv = (
+            v.__dict__[f"{x}{k}"] for x in ("bcat", "pown", "psend", "precv", "egive", "ekeep", "erecv")
+        )
         keep, give = share(k)
-        wide_out = ROWS + 128 if k < LEVELS - 1 else ROWS
 
         def product(rows):
             if k == 0:
                 return v.first[rows, :] + dot_nn(bcat[rows, 256:384], v.tmat[0, 256:384, :])
-            return dot_nn(bcat[rows, :], v.tmat[k, :, 0:wide_out])
-
-        there = {"wide": partners[k]}
-        pieces = []
+            return dot_nn(bcat[rows, :], v.tmat[k])
+
         p = product(give)
         psend[...] = p[:, 0:ROWS].astype(bf16)
-        if k < LEVELS - 1:
-            egive, ekeep, erecv = (v.__dict__[f"{x}{k}"] for x in ("egive", "ekeep", "erecv"))
-            egive[...] = p[:, ROWS:].astype(bf16)
-            pieces.append(remote(egive, erecv.at[2], {"wide": partners[k], "narrow": nxt}, has_next, has_prev))
-            pieces.append(remote(egive, erecv.at[3], {"wide": partners[k], "narrow": prv}, has_prev, has_next))
-        pieces.append(remote(psend, precv, there))
+        egive[...] = p[:, ROWS:].astype(bf16)
+        pieces = [
+            remote(egive, erecv.at[2], {"wide": partners[k], "narrow": nxt}, has_next, has_prev),
+            remote(egive, erecv.at[3], {"wide": partners[k], "narrow": prv}, has_prev, has_next),
+            remote(psend, precv, {"wide": partners[k]}),
+        ]
+        edge = egive
         if m < n:
             p = product(keep)
-            if k < LEVELS - 1:
-                ekeep[...] = p[:, ROWS:].astype(bf16)
-                edge = ekeep
-        elif k < LEVELS - 1:
-            edge = egive
-        if k < LEVELS - 1:
-            pieces.append(remote(edge, erecv.at[0], {"narrow": nxt}, has_next, has_prev))
-            pieces.append(remote(edge, erecv.at[1], {"narrow": prv}, has_prev, has_next))
+            ekeep[...] = p[:, ROWS:].astype(bf16)
+            edge = ekeep
+        pieces.append(remote(edge, erecv.at[0], {"narrow": nxt}, has_next, has_prev))
+        pieces.append(remote(edge, erecv.at[1], {"narrow": prv}, has_prev, has_next))
         pown[...] = p[:, 0:ROWS]
+        if k == 1:
+            last_t += [to_pieces(v.last_t, d) for d in (1, 3)]
+        if k == 2:
+            last_t.append(to_pieces(v.last_t, 2))
         idle_work(k)
         if k == SPLITS:
             for t in range(1, SPLITS):
@@ -397,23 +428,34 @@
         for item in pieces:
             arrived(item)
         total = pown[...] + precv[...].astype(f32)
-        if k < LEVELS - 1:
-            after = v.__dict__[f"bcat{k + 1}"]
-            v.__dict__[f"b32_{k + 1}"][...] = total
-            after[:, 0:256] = total.astype(bf16)
-            before = erecv[0].astype(f32) + erecv[2].astype(f32)
-            behind = erecv[1].astype(f32) + erecv[3].astype(f32)
-            side = lax.broadcasted_iota(jnp.int32, (m, 128), 1)
-            after[:, 256:384] = jnp.where(side < BS, before, behind).astype(bf16)
-        else:
-            v.b7[0] = total.astype(bf16)
-
-    gathers = [
-        remote(v.b7.at[0], v.b7.at[d], {"narrow": lax.rem(j + PIECES - d, PIECES)}) for d in (2, 1, 3)
+        after = v.__dict__[f"bcat{k + 1}"]
+        v.__dict__[f"b32_{k + 1}"][...] = total
+        after[:, 0:256] = total.astype(bf16)
+        before = erecv[0].astype(f32) + erecv[2].astype(f32)
+        behind = erecv[1].astype(f32) + erecv[3].astype(f32)
+        side = lax.broadcasted_iota(jnp.int32, (m, 128), 1)
+        after[:, 256:384] = jnp.where(side < BS, before, behind).astype(bf16)
+
+    k = JOINED
+    v.q_own[...] = dot_nn(v.bcat5[...], v.tmat[k, :, 0:256])
+    v.q_all[0] = v.q_own[...].astype(bf16)
+    gathers = [to_pieces(v.q_all, d) for d in (2, 1, 3)]
+    far = remote(v.q_all.at[0], v.q_far, {"wide": partners[k]})
+    idle_work(k)
+    v.x_own[...] = dot_nn(v.q_all[0], v.zmat[0])
+    for item in gathers:
+        arrived(item)
+    x = v.x_own[...]
+    for d in (1, 2, 3):
+        x = x + dot_nn(v.q_all[d], v.zmat[d])
+    v.x_send[...] = x.astype(bf16)
+    sums = [
+        remote(v.x_send, v.x_recv.at[i], {"wide": across(mask << k)}) for i, mask in enumerate((2, 3, 1))
     ]
-
-    def inverse_rows(d):
-        return v.kmat[pl.ds(pl.multiple_of(lax.rem(j + d, PIECES) * ROWS, ROWS), ROWS), :]
+    v.x_own[...] = x
+    arrived(far)
+    v.b32_6[...] = v.q_own[...] + v.q_far[...].astype(f32)
+    idle_work(LAST)
 
     b = v.b_std[...]
     dinv = jnp.concatenate([v.dcol[0]] * 4, axis=1)
@@ -425,12 +467,10 @@
             arrived(item)
         v.c_std[...] += dot_nt(v.fine[...], v.__dict__[f"cfull{t}"][...])
         v.fine[...] = dot_nn(v.fine[...], v.mmat[t]).astype(bf16)
-    v.ctot[...] += dot_nn(v.b7[0], inverse_rows(0))
-    for item in gathers:
+    for item in sums:
         arrived(item)
-    x = v.ctot[...]
-    for d in (1, 2, 3):
-        x = x + dot_nn(v.b7[d], inverse_rows(d))
+    x = v.x_own[...] + v.x_recv[0].astype(f32) + v.x_recv[1].astype(f32) + v.x_recv[2].astype(f32)
+    x = v.ctot[...] + dot_nn(x.astype(bf16), v.deep_t[...])
 
     rows = own_rows(SPLITS)
     v.xg[rows, :] = x.astype(bf16)

time: 63.8 us -> 60.5 us (0.948)
  Pallas kernels: 61.8 us -> 58.4 us
    pallas_call x1, Pallas kernels: 61.8 us -> 58.4 us  [on_device(): pl.pallas_call(kernel, out_shape=jax.ShapeDtypeStruct(rhs.shape, f32), in...]
where the time goes in v4:
time: 60.5 us; the launch traced here: 60.3 us
  Pallas kernels  58.4 us (97%)
  local copies, waits for them, and re-layouts  1.87 us (3%)
    pallas_call x1, Pallas kernels, on_device(): pl.pallas_call(kernel, out_shape=jax.ShapeDtypeStruct(rhs.shape, f32), in...  58.4 us
    unnamed x1, local copies, waits for them, and re-layouts  1.87 us

profile of v4, /device:TPU:1, one launch (start us, length us, event | category | flops | bytes accessed | tf_op | source)
XLA Modules:
  0.0 60.3 jit_solution(8000624887418674830)
XLA Ops:
  0.0 58.4 %shard_map.82 = f32[1,256,512]{2,1,0:T(8,128)} custom-call(s32[1,5,4,7]{3,2,1,0:T(4,128)} %bitcast.3, s32[1,3,4,7]{3,2,1,0:T(4,128)} %bitcast.4, s32[1,4,2,7]{3,2,1,0:T(2,128)} %bitcast.5, f32[1,256,512]{2,1,0:T(8,128)} %rhs_hbm.1, bf16[7,1,4,5,64,64]{5,4,3,2,1,0:T(8,128)(2,1)} %a_hbm.1, bf16[7,1,4,3,64,64]{5,4,3,2,1,0:T(8,128)(2,1)} %r_hbm.1, ...), custom_call_target="tpu_custom_call" | custom-call | tf_op jit(solution)/shard_map/pallas_call | solution.py:500
  58.4 1.9 %copy.10 = f32[1,256,512]{2,1,0:T(8,128)} copy(f32[1,256,512]{2,1,0:T(8,128)} %shard_map.82) | data formatting | bytes 1048576

commit v5 on v4

--- a/solution.py
+++ b/solution.py
@@ -74,9 +74,7 @@
         "x_send": vmem((FIELDS[LEVELS], ROWS), bf16),
         "x_recv": vmem((3, FIELDS[LEVELS], ROWS), bf16),
         "xg": vmem((ALL, ROWS), bf16),
-        "outv": vmem((ROWS, ALL), f32),
         "load_sem": dma((32,)),
-        "out_sem": dma((4,)),
         "send_sem": dma((REMOTES,)),
         "recv_sem": dma((REMOTES,)),
         "far_sem": pltpu.SemaphoreType.REGULAR((3, 2)),
@@ -91,9 +89,9 @@
             specs[f"pown{k}"] = vmem((m, ROWS), f32)
             specs[f"psend{k}"] = vmem((m, ROWS), bf16)
             specs[f"precv{k}"] = vmem((m, ROWS), bf16)
-            specs[f"egive{k}"] = vmem((m, 128), bf16)
-            specs[f"ekeep{k}"] = vmem((m, 128), bf16)
-            specs[f"erecv{k}"] = vmem((4, m, 128), bf16)
+            specs[f"egive{k}"] = vmem((2, m // 2, 128), bf16)
+            specs[f"ekeep{k}"] = vmem((2, m // 2, 128), bf16)
+            specs[f"erecv{k}"] = vmem((4, m // 2, 128), bf16)
         if 1 <= k < SPLITS:
             specs[f"cfull{k}"] = vmem((ALL, ROWS), bf16)
     return specs
@@ -103,7 +101,7 @@
     pass
 
 
-def kernel(gcol_hbm, rcol_hbm, pcol_hbm, rhs_hbm, a_hbm, r_hbm, p_hbm, inv_hbm, out_hbm, *refs):
+def kernel(gcol_hbm, rcol_hbm, pcol_hbm, rhs_hbm, a_hbm, r_hbm, p_hbm, inv_hbm, out, *refs):
     v = Refs()
     for name, ref in zip(scratch_specs(), refs):
         setattr(v, name, ref)
@@ -293,7 +291,7 @@
         v.dhalo[side] = jnp.zeros((LEVELS, 8, 128), f32)
         for k in range(JOINED):
             ref = v.__dict__[f"erecv{k}"]
-            zeros = jnp.zeros((FIELDS[k + 1], 128), bf16)
+            zeros = jnp.zeros((FIELDS[k + 1] // 2, 128), bf16)
             ref[side] = zeros
             ref[2 + side] = zeros
 
@@ -364,7 +362,7 @@
             v.deep[...] = dot_nn(v.deep[...], v.mmat[k]).astype(bf16)
         if k == JOINED - 1:
             ld_i.wait()
-            for item in last_t:
+            for item in handed_t:
                 arrived(item)
             join_last()
         if k == LAST:
@@ -383,7 +381,10 @@
     def to_pieces(ref, d):
         return remote(ref.at[0], ref.at[d], {"narrow": lax.rem(j + PIECES - d, PIECES)})
 
+    handed_t = []
     last_t = []
+    near = 1 + 2 * bits[0]
+    half = pl.ds(pl.multiple_of(bits[0] * (WIDE // 2), WIDE // 2), WIDE // 2)
     shared = {}
     for k in range(JOINED):
         n, m = FIELDS[k], FIELDS[k + 1]
@@ -399,25 +400,36 @@
 
         p = product(give)
         psend[...] = p[:, 0:ROWS].astype(bf16)
-        egive[...] = p[:, ROWS:].astype(bf16)
+        low = lax.broadcasted_iota(jnp.int32, (m // 2, 128), 1) < BS
+
+        def pack(ref, edge):
+            top, rolled = edge[0:m // 2], pltpu.roll(edge[m // 2:], BS, 1)
+            ref[0] = jnp.where(low, top, rolled).astype(bf16)
+            ref[1] = jnp.where(low, rolled, top).astype(bf16)
+
+        pack(egive, p[:, ROWS:])
         pieces = [
-            remote(egive, erecv.at[2], {"wide": partners[k], "narrow": nxt}, has_next, has_prev),
-            remote(egive, erecv.at[3], {"wide": partners[k], "narrow": prv}, has_prev, has_next),
+            remote(egive.at[0], erecv.at[2], {"wide": partners[k], "narrow": nxt}, has_next, has_prev),
+            remote(egive.at[1], erecv.at[3], {"wide": partners[k], "narrow": prv}, has_prev, has_next),
             remote(psend, precv, {"wide": partners[k]}),
         ]
         edge = egive
         if m < n:
             p = product(keep)
-            ekeep[...] = p[:, ROWS:].astype(bf16)
+            pack(ekeep, p[:, ROWS:])
             edge = ekeep
-        pieces.append(remote(edge, erecv.at[0], {"narrow": nxt}, has_next, has_prev))
-        pieces.append(remote(edge, erecv.at[1], {"narrow": prv}, has_prev, has_next))
+        pieces.append(remote(edge.at[0], erecv.at[0], {"narrow": nxt}, has_next, has_prev))
+        pieces.append(remote(edge.at[1], erecv.at[1], {"narrow": prv}, has_prev, has_next))
         pown[...] = p[:, 0:ROWS]
         if k == 1:
-            last_t += [to_pieces(v.last_t, d) for d in (1, 3)]
+            last_t.append(remote(v.last_t.at[0], v.last_t.at[near], {"narrow": lax.rem(j + PIECES - near, PIECES)}))
+            last_t.append(remote(v.last_t.at[0, half], v.last_t.at[2, half], {"narrow": lax.rem(j + 2, PIECES)}))
+        idle_work(k)
         if k == 2:
-            last_t.append(to_pieces(v.last_t, 2))
-        idle_work(k)
+            for item in last_t:
+                arrived(item)
+            handed_t.append(remote(v.last_t.at[near], v.last_t.at[near], {"wide": partners[0]}))
+            handed_t.append(remote(v.last_t.at[2, half], v.last_t.at[2, half], {"wide": partners[0]}))
         if k == SPLITS:
             for t in range(1, SPLITS):
                 rows = own_rows(t)
@@ -433,8 +445,8 @@
         after[:, 0:256] = total.astype(bf16)
         before = erecv[0].astype(f32) + erecv[2].astype(f32)
         behind = erecv[1].astype(f32) + erecv[3].astype(f32)
-        side = lax.broadcasted_iota(jnp.int32, (m, 128), 1)
-        after[:, 256:384] = jnp.where(side < BS, before, behind).astype(bf16)
+        after[0:m // 2, 256:384] = jnp.where(low, before, behind).astype(bf16)
+        after[m // 2:, 256:384] = pltpu.roll(jnp.where(low, behind, before), BS, 1).astype(bf16)
 
     k = JOINED
     v.q_own[...] = dot_nn(v.bcat5[...], v.tmat[k, :, 0:256])
@@ -479,29 +491,23 @@
     ]
     for item in handed:
         arrived(item)
-    outs = []
     for c in range(4):
         cols = slice(c * 128, (c + 1) * 128)
-        v.outv[:, cols] = v.c_std[:, cols] + dot_nt(v.fine[...], v.xg[cols, :])
-        copy = pltpu.make_async_copy(v.outv.at[:, cols], out_hbm.at[0, :, cols], v.out_sem.at[c])
-        copy.start()
-        outs.append(copy)
+        out[0, :, cols] = v.c_std[:, cols] + dot_nt(v.fine[...], v.xg[cols, :])
     for copy, sends in started:
         if sends is None:
             copy.wait_send()
         else:
             pl.when(sends)(copy.wait_send)
-    for copy in outs:
-        copy.wait()
 
 
 def on_device(rhs, gcol, galerkin, rcol, restrict, pcol, prolong, inverse):
     hbm = pl.BlockSpec(memory_space=pl.ANY)
     return pl.pallas_call(
         kernel,
-        out_shape=jax.ShapeDtypeStruct(rhs.shape, f32),
+        out_shape=pltpu.VMEM(rhs.shape, f32),
         in_specs=[hbm] * 8,
-        out_specs=hbm,
+        out_specs=pl.BlockSpec(memory_space=pltpu.VMEM),
         scratch_shapes=list(scratch_specs().values()),
         compiler_params=pltpu.CompilerParams(
             collective_id=0, has_side_effects=True, vmem_limit_bytes=60 * 1024 * 1024

time: 60.5 us -> 56.4 us (0.932)
  Pallas kernels: 58.4 us -> 55.5 us
  local copies, waits for them, and re-layouts: 1.87 us -> 0.8 us
    pallas_call x1, Pallas kernels: 58.4 us -> 55.5 us  [on_device(): pl.pallas_call(kernel, out_shape=pltpu.VMEM(rhs.shape, f32), in_specs=[hb...]
    unnamed x1, local copies, waits for them, and re-layouts: 1.87 us -> 0.8 us
where the time goes in v5:
time: 56.4 us; the launch traced here: 56.3 us
  Pallas kernels  55.5 us (98%)
  local copies, waits for them, and re-layouts  0.8 us (1%)
    pallas_call x1, Pallas kernels, on_device(): pl.pallas_call(kernel, out_shape=pltpu.VMEM(rhs.shape, f32), in_specs=[hb...  55.5 us

profile of v5, /device:TPU:1, one launch (start us, length us, event | category | flops | bytes accessed | tf_op | source)
XLA Modules:
  0.0 56.3 jit_solution(8568684855683196252)
XLA Ops:
  0.0 55.5 %shard_map.82 = f32[1,256,512]{2,1,0:T(8,128)S(1)} custom-call(s32[1,5,4,7]{3,2,1,0:T(4,128)} %bitcast.3, s32[1,3,4,7]{3,2,1,0:T(4,128)} %bitcast.4, s32[1,4,2,7]{3,2,1,0:T(2,128)} %bitcast.5, f32[1,256,512]{2,1,0:T(8,128)} %rhs_hbm.1, bf16[7,1,4,5,64,64]{5,4,3,2,1,0:T(8,128)(2,1)} %a_hbm.1, bf16[7,1,4,3,64,64]{5,4,3,2,1,0:T(8,128)(2,1)} %r_hbm.1, ...), custom_call_target="tpu_custom_call" | custom-call | tf_op jit(solution)/shard_map/pallas_call | solution.py:506
  55.5 0.8 %copy.10 = f32[1,256,512]{2,1,0:T(8,128)} copy(f32[1,256,512]{2,1,0:T(8,128)S(1)} %shard_map.82) | data formatting | bytes 1048576

commit v6 on v5

--- a/solution.py
+++ b/solution.py
@@ -54,6 +54,8 @@
         "fine": vmem((ROWS, ROWS), bf16),
         "deep_t": vmem((ROWS, ROWS), bf16),
         "last_t": vmem((PIECES, WIDE, ROWS), bf16),
+        "join_t": vmem((PIECES, WIDE, ROWS), bf16),
+        "q_next": vmem((FIELDS[LEVELS], ROWS), bf16),
         "zpart": vmem((PIECES, WIDE, ROWS), f32),
         "zmat": vmem((PIECES, ROWS, ROWS), bf16),
         "drow": vmem((LEVELS, 8, ROWS), f32),
@@ -72,7 +74,7 @@
         "q_far": vmem((FIELDS[LEVELS], ROWS), bf16),
         "x_own": vmem((FIELDS[LEVELS], ROWS), f32),
         "x_send": vmem((FIELDS[LEVELS], ROWS), bf16),
-        "x_recv": vmem((3, FIELDS[LEVELS], ROWS), bf16),
+        "x_recv": vmem((7, FIELDS[LEVELS], ROWS), bf16),
         "xg": vmem((ALL, ROWS), bf16),
         "load_sem": dma((32,)),
         "send_sem": dma((REMOTES,)),
@@ -192,6 +194,18 @@
             copy.wait_recv()
         else:
             pl.when(recvs)(copy.wait_recv)
+
+    def all_arrived(items):
+        for copy, recvs in items:
+            if recvs is None:
+                copy.wait_recv()
+        for side in (has_prev, has_next):
+            def wait_side():
+                for copy, recvs in items:
+                    if recvs is side:
+                        copy.wait_recv()
+
+            pl.when(side)(wait_side)
 
     lane = lax.broadcasted_iota(jnp.int32, (BS, 2 * BS), 1)
     row = lax.broadcasted_iota(jnp.int32, (BS, 2 * BS), 0)
@@ -342,11 +356,15 @@
             ld_r.wait()
             for item in diags:
                 arrived(item)
-        if k + 1 < LAST:
-            prep_t(k + 1)
         if k == 0:
             prep_t(LAST)
             v.last_t[0] = v.tmat[LAST, :, 0:256]
+            last_t.extend([fetch(v.last_t, True), fetch(v.last_t, False)])
+        if k + 1 < JOINED:
+            prep_t(k + 1)
+        if k == 0:
+            prep_t(JOINED)
+            v.join_t[0] = v.tmat[JOINED, :, 0:256]
         if k == 0:
             ld_pc.wait()
             ld_p.wait()
@@ -360,18 +378,25 @@
         if k > SPLITS:
             v.ctot[...] += dot_nt(smoothed_twice(k).astype(bf16), v.deep[...])
             v.deep[...] = dot_nn(v.deep[...], v.mmat[k]).astype(bf16)
-        if k == JOINED - 1:
+        if k == JOINED - 2:
             ld_i.wait()
             for item in handed_t:
                 arrived(item)
-            join_last()
+            join(v.last_t, False)
+        if k == JOINED - 1:
+            for item in handed_j:
+                arrived(item)
+            join(v.join_t, True)
         if k == LAST:
             v.deep_t[...] = jnp.transpose(v.deep[...].astype(f32)).astype(bf16)
 
-    def join_last():
+    def join(matrices, further):
         for d in range(PIECES):
+            if further:
+                v.zpart[d] = dot_nn(matrices[d], v.zmat[d])
+                continue
             cols = pl.ds(pl.multiple_of(lax.rem(j + d, PIECES) * ROWS, ROWS), ROWS)
-            v.zpart[d] = dot_nt(v.last_t[d], v.cinv[:, cols])
+            v.zpart[d] = dot_nt(matrices[d], v.cinv[:, cols])
         for d in range(PIECES):
             before, after = (d + PIECES - 1) % PIECES, (d + 1) % PIECES
             v.zmat[d, 0:64, :] = (v.zpart[d, 0:64, :] + v.zpart[before, 320:384, :]).astype(bf16)
@@ -382,7 +407,19 @@
         return remote(ref.at[0], ref.at[d], {"narrow": lax.rem(j + PIECES - d, PIECES)})
 
     handed_t = []
+    handed_j = []
     last_t = []
+    join_t = []
+
+    def fetch(ref, whole):
+        if whole:
+            return remote(ref.at[0], ref.at[near], {"narrow": lax.rem(j + PIECES - near, PIECES)})
+        return remote(ref.at[0, half], ref.at[2, half], {"narrow": lax.rem(j + 2, PIECES)})
+
+    def hand(ref, whole):
+        part = ref.at[near] if whole else ref.at[2, half]
+        return remote(part, part, {"wide": partners[0]})
+
     near = 1 + 2 * bits[0]
     half = pl.ds(pl.multiple_of(bits[0] * (WIDE // 2), WIDE // 2), WIDE // 2)
     shared = {}
@@ -400,6 +437,9 @@
 
         p = product(give)
         psend[...] = p[:, 0:ROWS].astype(bf16)
+        if k == JOINED - 1:
+            v.q_all[0] = psend[...]
+            gathers = [to_pieces(v.q_all, d) for d in (2, 1, 3)]
         low = lax.broadcasted_iota(jnp.int32, (m // 2, 128), 1) < BS
 
         def pack(ref, edge):
@@ -422,14 +462,18 @@
         pieces.append(remote(edge.at[1], erecv.at[1], {"narrow": prv}, has_prev, has_next))
         pown[...] = p[:, 0:ROWS]
         if k == 1:
-            last_t.append(remote(v.last_t.at[0], v.last_t.at[near], {"narrow": lax.rem(j + PIECES - near, PIECES)}))
-            last_t.append(remote(v.last_t.at[0, half], v.last_t.at[2, half], {"narrow": lax.rem(j + 2, PIECES)}))
+            join_t.append(fetch(v.join_t, True))
+        if k == 3:
+            join_t.append(fetch(v.join_t, False))
+        if k == JOINED - 1:
+            for item in join_t:
+                arrived(item)
+            handed_j += [hand(v.join_t, True), hand(v.join_t, False)]
         idle_work(k)
         if k == 2:
             for item in last_t:
                 arrived(item)
-            handed_t.append(remote(v.last_t.at[near], v.last_t.at[near], {"wide": partners[0]}))
-            handed_t.append(remote(v.last_t.at[2, half], v.last_t.at[2, half], {"wide": partners[0]}))
+            handed_t += [hand(v.last_t, True), hand(v.last_t, False)]
         if k == SPLITS:
             for t in range(1, SPLITS):
                 rows = own_rows(t)
@@ -437,8 +481,20 @@
                 shared[t] = [
                     remote(ref.at[rows], ref.at[rows], {"wide": across(mask)}) for mask in range(1, 1 << t)
                 ]
-        for item in pieces:
-            arrived(item)
+        if k == JOINED - 1:
+            v.x_own[...] = dot_nn(v.q_all[0], v.zmat[0])
+            for item in gathers:
+                arrived(item)
+            x = v.x_own[...]
+            for d in (1, 2, 3):
+                x = x + dot_nn(v.q_all[d], v.zmat[d])
+            v.x_send[...] = x.astype(bf16)
+            sums = [
+                remote(v.x_send, v.x_recv.at[i], {"wide": across(mask << k)})
+                for i, mask in enumerate((4, 5, 3, 6, 2, 7, 1))
+            ]
+            v.x_own[...] = x
+        all_arrived(pieces)
         total = pown[...] + precv[...].astype(f32)
         after = v.__dict__[f"bcat{k + 1}"]
         v.__dict__[f"b32_{k + 1}"][...] = total
@@ -450,24 +506,9 @@
 
     k = JOINED
     v.q_own[...] = dot_nn(v.bcat5[...], v.tmat[k, :, 0:256])
-    v.q_all[0] = v.q_own[...].astype(bf16)
-    gathers = [to_pieces(v.q_all, d) for d in (2, 1, 3)]
-    far = remote(v.q_all.at[0], v.q_far, {"wide": partners[k]})
+    v.q_next[...] = v.q_own[...].astype(bf16)
+    far = remote(v.q_next, v.q_far, {"wide": partners[k]})
     idle_work(k)
-    v.x_own[...] = dot_nn(v.q_all[0], v.zmat[0])
-    for item in gathers:
-        arrived(item)
-    x = v.x_own[...]
-    for d in (1, 2, 3):
-        x = x + dot_nn(v.q_all[d], v.zmat[d])
-    v.x_send[...] = x.astype(bf16)
-    sums = [
-        remote(v.x_send, v.x_recv.at[i], {"wide": across(mask << k)}) for i, mask in enumerate((2, 3, 1))
-    ]
-    v.x_own[...] = x
-    arrived(far)
-    v.b32_6[...] = v.q_own[...] + v.q_far[...].astype(f32)
-    idle_work(LAST)
 
     b = v.b_std[...]
     dinv = jnp.concatenate([v.dcol[0]] * 4, axis=1)
@@ -479,9 +520,14 @@
             arrived(item)
         v.c_std[...] += dot_nt(v.fine[...], v.__dict__[f"cfull{t}"][...])
         v.fine[...] = dot_nn(v.fine[...], v.mmat[t]).astype(bf16)
+    arrived(far)
+    v.b32_6[...] = v.q_own[...] + v.q_far[...].astype(f32)
+    idle_work(LAST)
     for item in sums:
         arrived(item)
-    x = v.x_own[...] + v.x_recv[0].astype(f32) + v.x_recv[1].astype(f32) + v.x_recv[2].astype(f32)
+    x = v.x_own[...]
+    for i in range(7):
+        x = x + v.x_recv[i].astype(f32)
     x = v.ctot[...] + dot_nn(x.astype(bf16), v.deep_t[...])
 
     rows = own_rows(SPLITS)

time: 56.4 us -> 55.6 us (0.986)
  Pallas kernels: 55.5 us -> 54.6 us
    pallas_call x1, Pallas kernels: 55.5 us -> 54.6 us  [on_device(): pl.pallas_call(kernel, out_shape=pltpu.VMEM(rhs.shape, f32), in_specs=[hb...]
where the time goes in v6:
time: 55.6 us; the launch traced here: 55.4 us
  Pallas kernels  54.6 us (98%)
  local copies, waits for them, and re-layouts  0.8 us (1%)
    pallas_call x1, Pallas kernels, on_device(): pl.pallas_call(kernel, out_shape=pltpu.VMEM(rhs.shape, f32), in_specs=[hb...  54.6 us

profile of v6, /device:TPU:1, one launch (start us, length us, event | category | flops | bytes accessed | tf_op | source)
XLA Modules:
  0.0 55.4 jit_solution(7286840038489906697)
XLA Ops:
  0.0 54.6 %shard_map.82 = f32[1,256,512]{2,1,0:T(8,128)S(1)} custom-call(s32[1,5,4,7]{3,2,1,0:T(4,128)} %bitcast.3, s32[1,3,4,7]{3,2,1,0:T(4,128)} %bitcast.4, s32[1,4,2,7]{3,2,1,0:T(2,128)} %bitcast.5, f32[1,256,512]{2,1,0:T(8,128)} %rhs_hbm.1, bf16[7,1,4,5,64,64]{5,4,3,2,1,0:T(8,128)(2,1)} %a_hbm.1, bf16[7,1,4,3,64,64]{5,4,3,2,1,0:T(8,128)(2,1)} %r_hbm.1, ...), custom_call_target="tpu_custom_call" | custom-call | tf_op jit(solution)/shard_map/pallas_call | solution.py:552
  54.6 0.8 %copy.10 = f32[1,256,512]{2,1,0:T(8,128)} copy(f32[1,256,512]{2,1,0:T(8,128)S(1)} %shard_map.82) | data formatting | bytes 1048576

commit v7 on v6

--- a/solution.py
+++ b/solution.py
@@ -130,8 +130,9 @@
         return lax.rem(w + distance, size), lax.rem(w + size - distance, size)
 
     barrier = pltpu.get_barrier_semaphore()
-    greeted = [{"narrow": lax.rem(j + d, PIECES)} for d in (1, 2, 3)]
-    greeted += [{"wide": p} for p in partners[:3]]
+    y = lax.rem(w // 2, 4)
+    greeted = [{"narrow": nxt}, {"narrow": prv}, {"wide": partners[0]}]
+    greeted += [{"wide": w + 2 * (lax.rem(y + d, 4) - y)} for d in (1, 3)]
     greeted += [{"wide": p} for p in ring(8)]
     for where in greeted:
         pl.semaphore_signal(barrier, inc=1, device_id=where)

time: 55.6 us -> 55.6 us (level)
  no operation moved by 1% of the time
where the time goes in v7:
time: 55.6 us; the launch traced here: 55.4 us
  Pallas kernels  54.6 us (98%)
  local copies, waits for them, and re-layouts  0.8 us (1%)
    pallas_call x1, Pallas kernels, on_device(): pl.pallas_call(kernel, out_shape=pltpu.VMEM(rhs.shape, f32), in_specs=[hb...  54.6 us

profile of v7, /device:TPU:1, one launch (start us, length us, event | category | flops | bytes accessed | tf_op | source)
XLA Modules:
  0.0 55.4 jit_solution(8711461897293168829)
XLA Ops:
  0.0 54.6 %shard_map.82 = f32[1,256,512]{2,1,0:T(8,128)S(1)} custom-call(s32[1,5,4,7]{3,2,1,0:T(4,128)} %bitcast.3, s32[1,3,4,7]{3,2,1,0:T(4,128)} %bitcast.4, s32[1,4,2,7]{3,2,1,0:T(2,128)} %bitcast.5, f32[1,256,512]{2,1,0:T(8,128)} %rhs_hbm.1, bf16[7,1,4,5,64,64]{5,4,3,2,1,0:T(8,128)(2,1)} %a_hbm.1, bf16[7,1,4,3,64,64]{5,4,3,2,1,0:T(8,128)(2,1)} %r_hbm.1, ...), custom_call_target="tpu_custom_call" | custom-call | tf_op jit(solution)/shard_map/pallas_call | solution.py:553
  54.6 0.8 %copy.10 = f32[1,256,512]{2,1,0:T(8,128)} copy(f32[1,256,512]{2,1,0:T(8,128)S(1)} %shard_map.82) | data formatting | bytes 1048576
